TPU v7x, 32 devices: a whole 2x2x4 slice. The times are simulated.
32 devices in a mesh: band: 8 (over z, y), lev: 4 (over x, core).
Axes of the slice: x: 2, y: 2, z: 4, core: 2. Of those that a mesh axis runs over, the one named last changes fastest.
Arguments:
- grid_adjoint: float32 [1024, 64, 2048], P('band', 'lev'), may hold values from -6 to 6
- trajectory: float32 [1024, 64, 2048], P('band', 'lev'), may hold values from -3 to 3
- legendre_north: float32 [512, 512, 512], P(('band', 'lev')), may hold values from -0.25 to 0.25
- slot_wavenumber: int32 [512], replicated, may hold values from 0 to 511, each once
- spectral_state: float32 [512, 512, 2, 64], P(('band', 'lev')), may hold values from -6 to 6
- to_modes: float32 [64, 64], replicated, may hold values from -0.75 to 0.75
- from_modes: float32 [64, 64], replicated, may hold values from -0.75 to 0.75
- rates: float32 [64], replicated, may hold values from 0.1 to 10
Outputs:
- spectral_out: float32 [512, 512, 2, 64], P(('band', 'lev'))
- grid_out: float32 [1024, 64, 2048], P('band', 'lev')
Inputs may be any that keep to these rules, and one draw needn't show every extreme that they name: `slot_wavenumber`: each wavenumber stands in exactly one slot.
All inputs are finite; a program needn't handle non-finite values.
Results may differ from a plain program's by a relative error of at most 0.000067.
Values sent between devices are 32-bit elements; how exact they have to be, the bound alone decides.
A program may use at most 192 MiB of HBM per device.

v0:
```python
import jax
import jax.numpy as jnp
from jax import lax
from jax.sharding import PartitionSpec as P

PRECISION = lax.Precision.HIGH


def angle_parts(steps, waves, longitudes):
    phase = waves[:, None] * steps[None, :] % longitudes
    angles = phase.astype(jnp.float32) * (2.0 * jnp.pi / longitudes)
    return jnp.cos(angles), jnp.sin(angles)


def wave_rows(longitudes, waves, devices):
    fine = min(128, longitudes)
    coarse = longitudes // fine
    scale = jnp.float32(longitudes) ** (-0.5)
    cos_a, sin_a = angle_parts(jnp.arange(coarse, dtype=jnp.int32) * fine, waves, longitudes)
    cos_b, sin_b = angle_parts(jnp.arange(fine, dtype=jnp.int32), waves, longitudes)
    cos_a, sin_a, cos_b, sin_b = lax.optimization_barrier(
        (cos_a * scale, sin_a * scale, cos_b, sin_b)
    )
    cos_at = [cos_a[:, i : i + 1] * cos_b - sin_a[:, i : i + 1] * sin_b for i in range(coarse)]
    sin_at = [-sin_a[:, i : i + 1] * cos_b - cos_a[:, i : i + 1] * sin_b for i in range(coarse)]
    cosine = jnp.concatenate(cos_at, axis=1).reshape(devices, -1, longitudes)
    negsine = jnp.concatenate(sin_at, axis=1).reshape(devices, -1, longitudes)
    return jnp.stack([cosine, negsine], axis=1).reshape(-1, longitudes)


def exchange(data):
    return lax.all_to_all(data, ("band", "lev"), split_axis=0, concat_axis=0, tiled=True)


def shards(
    grid_adjoint,
    trajectory,
    legendre_north,
    slot_wavenumber,
    spectral_state,
    to_modes,
    from_modes,
    rates,
):
    lats, levels, longitudes = grid_adjoint.shape
    slots, depth, half = legendre_north.shape
    bands = lax.axis_size("band")
    parts = lax.axis_size("lev")
    devices = bands * parts
    every = parts * levels
    me = lax.axis_index("band") * parts + lax.axis_index("lev")
    own_waves = lax.dynamic_slice_in_dim(slot_wavenumber, me * slots, slots)
    table = wave_rows(longitudes, slot_wavenumber, devices)
    even_k = jnp.arange(depth, dtype=jnp.int32) % 2 == 0

    forced = grid_adjoint * (1.0 + trajectory)
    rows = jnp.swapaxes(forced, 0, 1).reshape(levels * lats, longitudes)
    fourier = lax.dot_general(
        table, rows, (((1,), (1,)), ((), ())), precision=PRECISION, preferred_element_type=jnp.float32
    )
    arrived = exchange(fourier.reshape(devices, 2 * slots, levels * lats))
    arrived = arrived.reshape(bands, parts, 2, slots, levels, lats)
    arrived = arrived.transpose(3, 2, 1, 4, 0, 5).reshape(slots, 2 * every, bands * lats)
    north = arrived[:, :, :half]
    south = arrived[:, :, half:][:, :, ::-1]
    folded = jnp.concatenate([north + south, north - south], axis=1)
    both = lax.dot_general(
        folded, legendre_north, (((2,), (2,)), ((0,), (0,))), precision=PRECISION,
        preferred_element_type=jnp.float32,
    )
    analysed = jnp.where(even_k, both[:, : 2 * every], both[:, 2 * every :])
    analysed = analysed.reshape(slots, 2, every, depth)

    state = spectral_state.transpose(0, 2, 3, 1)
    depth_index = jnp.arange(depth, dtype=jnp.int32)
    valid = (depth_index[None, :] < depth - own_waves[:, None]).astype(jnp.float32)
    total = (analysed + state) * valid[:, None, None, :]
    degree = (own_waves[:, None] + depth_index[None, :]).astype(jnp.float32)
    helm = degree * (degree + 1.0) / (depth * (depth - 1.0))
    modes = jnp.einsum("sclk,pl->scpk", total, to_modes, precision=PRECISION)
    scaled = modes / (1.0 + helm[:, None, None, :] * rates[None, None, :, None])
    spectral = jnp.einsum("scpk,lp->sclk", scaled, from_modes, precision=PRECISION)

    coeffs = spectral.reshape(slots, 2 * every, depth)
    split = jnp.concatenate(
        [jnp.where(even_k, coeffs, 0.0), jnp.where(even_k, 0.0, coeffs)], axis=1
    )
    halves = lax.dot_general(
        split, legendre_north, (((2,), (1,)), ((0,), (0,))), precision=PRECISION,
        preferred_element_type=jnp.float32,
    )
    first = halves[:, : 2 * every]
    second = halves[:, 2 * every :]
    whole = jnp.concatenate([first + second, (first - second)[:, :, ::-1]], axis=2)
    whole = whole.reshape(slots, 2, parts, levels, bands, lats).transpose(4, 2, 1, 0, 3, 5)
    returned = exchange(whole.reshape(devices, 2 * slots, levels * lats))
    grid = lax.dot_general(
        returned.reshape(devices * 2 * slots, levels, lats),
        table,
        (((0,), (0,)), ((), ())),
        precision=PRECISION,
        preferred_element_type=jnp.float32,
    )
    return spectral.transpose(0, 3, 1, 2), jnp.swapaxes(grid, 0, 1)


def solution(mesh):
    return jax.shard_map(
        shards,
        mesh=mesh,
        in_specs=(
            P("band", "lev", None),
            P("band", "lev", None),
            P(("band", "lev"), None, None),
            P(),
            P(("band", "lev"), None, None, None),
            P(),
            P(),
            P(),
        ),
        out_specs=(P(("band", "lev"), None, None, None), P("band", "lev", None)),
        check_vma=False,
    )
```

profile of v0, /device:TPU:0, one launch (start us, length us, event | category | flops | bytes accessed | tf_op | source)
XLA Modules:
  0.0 703.2 jit_solution(9347582182654225411)
XLA Ops:
  0.6 0.0 copy-start
  0.7 1.8 fusion.25
  2.4 0.9 sine_multiply_fusion
  3.4 0.3 subtract_dynamic-update-slice_fusion.31
  3.7 0.3 subtract_dynamic-update-slice_fusion.30
  4.0 0.3 subtract_dynamic-update-slice_fusion.29
  4.3 0.0 slice-start
  4.3 0.3 subtract_dynamic-update-slice_fusion.28
  4.6 0.3 subtract_dynamic-update-slice_fusion.27
  4.8 0.3 subtract_dynamic-update-slice_fusion.26
  5.1 0.3 subtract_dynamic-update-slice_fusion.25
  5.4 0.3 subtract_dynamic-update-slice_fusion.24
  5.7 0.3 subtract_dynamic-update-slice_fusion.23
  6.0 0.3 subtract_dynamic-update-slice_fusion.22
  6.2 0.0 slice-start.1
  6.2 0.3 subtract_dynamic-update-slice_fusion.21
  6.5 0.3 subtract_dynamic-update-slice_fusion.20
  6.8 0.3 subtract_dynamic-update-slice_fusion.19
  7.1 0.3 subtract_dynamic-update-slice_fusion.18
  7.4 0.3 subtract_dynamic-update-slice_fusion.17
  7.6 0.3 subtract_dynamic-update-slice_fusion.16
  7.9 0.0 copy-start.2
  7.9 2.0 copy-done.2
  9.9 6.6 pad_maximum_fusion
  16.5 0.0 slice-done
  16.5 0.0 slice-done.1
  16.5 0.0 slice-done.2
  16.5 0.0 slice-done.3
  16.5 27.3 %copy_multiply_fusion = f32[128,16,2048]{2,0,1:T(8,128)} fusion(f32[128,16,2048]{2,1,0:T(8,128)S(1)} %bitcast.117, f32[128,16,2048]{2,1,0:T(8,128)} %param.9), kind=kLoop, calls=%fused_computation | loop fusion | flops 8388608 | bytes 50331648 | tf_op jit(solution)/shard_map/mul | solution.py:56
  43.9 33.2 %fusion.43 = f32[32,32,2048]{2,1,0:T(8,128)} fusion(f32[32,32,2048]{2,1,0:T(8,128)} %bitcast.120, f32[2048,2048,1]{1,0,2:T(8,128)} %bitcast.118), kind=kOutput, calls=%fused_computation.119 | convolution fusion | flops 25769803776 | bytes 33554432 | tf_op jit(solution)/shard_map/dot_general | solution.py:58
  77.0 7.9 %all-to-all-start = ((f32[32,32,2048]{2,1,0:T(8,128)}), f32[32,32,2048]{2,1,0:T(8,128)}, u32[]{:S(2)}, u32[]{:S(2)}) async-start(f32[32,32,2048]{2,1,0:T(8,128)} %fusion.43), calls=%async_computation | async-start | bytes 16777216 | tf_op jit(solution)/shard_map/all_to_all | solution.py:32
  84.9 0.8 broadcast_subtract_fusion
  85.7 0.1 fusion.33
  85.8 0.1 fusion.29
  85.8 0.0 copy-done.5
  85.9 0.3 multiply_add_fusion
  86.2 184.6 %all-to-all-done = f32[32,32,2048]{2,1,0:T(8,128)} async-done(((f32[32,32,2048]{2,1,0:T(8,128)}), f32[32,32,2048]{2,1,0:T(8,128)}, u32[]{:S(2)}, u32[]{:S(2)}) %all-to-all-start) | async-done | bytes 8388640 | tf_op jit(solution)/shard_map/all_to_all | solution.py:32
  270.8 5.4 copy.20
  276.2 8.3 %copy.14 = f32[16,2,4,16,8,128]{5,4,3,2,1,0:T(8,128)} copy(f32[16,2,4,16,8,128]{5,3,0,1,2,4:T(8,128)S(1)} %bitcast.112) | data formatting | bytes 16777216 | tf_op jit(solution)/shard_map/transpose | solution.py:63
  284.4 9.2 %reshape.90 = f32[16,128,1024]{2,1,0:T(8,128)} reshape(f32[16,2,4,16,8,128]{5,4,3,2,1,0:T(8,128)} %copy.14) | data formatting | bytes 16777216 | tf_op jit(solution)/shard_map/reshape | solution.py:63
  293.7 4.8 slice.185
  298.5 34.2 %rev.6 = f32[16,128,512]{2,1,0:T(8,128)} reverse(f32[16,128,512]{2,1,0:T(8,128)} %slice.185), dimensions={2} | reverse | bytes 8388608 | tf_op jit(solution)/shard_map/rev | solution.py:65
  332.7 8.4 %slice_add_fusion.1 = (f32[16,128,512]{2,1,0:T(8,128)}, f32[16,128,512]{2,1,0:T(8,128)}) fusion(f32[16,128,512]{2,1,0:T(8,128)} %rev.6, f32[16,128,1024]{2,1,0:T(8,128)} %reshape.90), kind=kLoop, calls=%fused_computation.27 | loop fusion | flops 2097152 | bytes 16777216 | tf_op jit(solution)/shard_map/add | solution.py:66
  341.1 14.3 %fusion = f32[16,256,512]{2,1,0:T(8,128)} fusion(f32[16,512,512]{2,1,0:T(8,128)} %param.10, f32[16,128,512]{2,1,0:T(8,128)} %get-tuple-element.17, f32[16,128,512]{2,1,0:T(8,128)} %get-tuple-element.16), kind=kOutput, calls=%fused_computation.3 | convolution fusion | flops 6444548096 | bytes 33554432 | tf_op jit(solution)/shard_map/dot_general | solution.py:67
  355.4 4.6 slice_select_fusion
  360.1 0.0 copy-start.6
  360.1 2.9 fusion.15
  363.0 0.0 copy-done.6
  363.1 2.5 fusion.13
  365.6 0.0 copy-start.4
  365.6 4.6 bitcast_select_fusion.1
  370.2 15.1 %fusion.4 = f32[16,256,512]{2,1,0:T(8,128)} fusion(f32[16,512,512]{2,1,0:T(8,128)} %param.10, f32[16,128,512]{2,1,0:T(8,128)} %get-tuple-element.21, f32[16,128,512]{2,1,0:T(8,128)} %get-tuple-element.20), kind=kOutput, calls=%fused_computation.7 | convolution fusion | flops 6444548096 | bytes 33554432 | tf_op jit(solution)/shard_map/dot_general | solution.py:88
  385.2 8.3 %slice_add_fusion = (f32[16,128,512]{2,1,0:T(8,128)}, f32[16,128,512]{2,1,0:T(8,128)}) fusion(f32[16,256,512]{2,1,0:T(8,128)} %fusion.4), kind=kLoop, calls=%fused_computation.25 | loop fusion | flops 2097152 | bytes 16777216 | tf_op jit(solution)/shard_map/add | solution.py:94
  393.6 34.2 %rev.7 = f32[16,128,512]{2,1,0:T(8,128)} reverse(f32[16,128,512]{2,1,0:T(8,128)} %get-tuple-element.19), dimensions={2} | reverse | bytes 8388608 | tf_op jit(solution)/shard_map/rev | solution.py:94
  427.8 4.5 pad_maximum_fusion.1
  432.3 5.5 copy.21
  437.8 8.3 %copy.32 = f32[16,2,4,16,8,128]{5,3,0,1,2,4:T(8,128)} copy(f32[16,2,4,16,8,128]{5,4,3,2,1,0:T(8,128)} %bitcast.113) | data formatting | bytes 16777216 | tf_op jit(solution)/shard_map/reshape | solution.py:95
  446.1 9.2 %reshape.94 = f32[32,32,2048]{2,1,0:T(8,128)} reshape(f32[8,4,2,16,16,128]{5,4,3,2,1,0:T(8,128)} %bitcast.114) | data formatting | bytes 16777216 | tf_op jit(solution)/shard_map/reshape | solution.py:96
  455.3 186.6 %all_to_all.10 = f32[32,32,2048]{2,1,0:T(8,128)S(1)} all-to-all(f32[32,32,2048]{2,1,0:T(8,128)} %reshape.94), channel_id=1, replica_groups=mesh['band'=8,'lev'=4] {'band','lev'}, dimensions={0} | all-to-all | bytes 16777216 | tf_op jit(solution)/shard_map/all_to_all | solution.py:32
  641.9 5.4 copy.22
  647.2 35.7 %fusion.10 = f32[128,16,2048]{2,0,1:T(8,128)S(1)} fusion(f32[1024,2048,1]{1,0,2:T(8,128)} %bitcast.121, f32[1024,16,128]{2,1,0:T(8,128)} %bitcast.122), kind=kOutput, calls=%fused_computation.15 | convolution fusion | flops 25769803776 | bytes 33554432 | tf_op jit(solution)/shard_map/dot_general | solution.py:97
  682.9 0.0 copy-start.1
  682.9 19.8 %copy.17 = f32[128,16,2048]{2,1,0:T(8,128)} copy(f32[128,16,2048]{2,0,1:T(8,128)S(1)} %fusion.10) | data formatting | bytes 33554432
  702.7 0.0 copy-done.1
  (13 shorter events, 0.1 us)
Async XLA Ops:
  0.6 359.5 %copy-start = (f32[64,64]{1,0:T(8,128)S(1)}, f32[64,64]{1,0:T(8,128)}, u32[]{:S(2)}) copy-start(f32[64,64]{1,0:T(8,128)} %param.13) | copy-start | bytes 49156
  4.3 12.2 %slice-start = ((s8[16777216]{0:T(1024)(128)(4,1)}), s8[4194304]{0:T(1024)(128)(4,1)S(1)}, s32[]{:S(2)}) async-start(s8[16777216]{0:T(1024)(128)(4,1)} %bitcast.116), calls=%async_computation.2 | async-start | bytes 8388608
  6.2 10.3 %slice-start.1 = ((s8[16777216]{0:T(1024)(128)(4,1)}), s8[4194304]{0:T(1024)(128)(4,1)S(1)}, s32[]{:S(2)}) async-start(s8[16777216]{0:T(1024)(128)(4,1)} %bitcast.116), calls=%async_computation.3 | async-start | bytes 8388608
  7.9 2.0 copy-start.2
  9.9 6.6 slice-start.2
  9.9 6.6 slice-start.3
  77.0 8.8 %copy-start.5 = (f32[64]{0:T(128)S(1)}, f32[64]{0:T(128)}, u32[]{:S(2)}) copy-start(f32[64]{0:T(128)} %param.15) | copy-start | bytes 772
  77.0 193.7 %all-to-all-start = ((f32[32,32,2048]{2,1,0:T(8,128)}), f32[32,32,2048]{2,1,0:T(8,128)}, u32[]{:S(2)}, u32[]{:S(2)}) async-start(f32[32,32,2048]{2,1,0:T(8,128)} %fusion.43), calls=%async_computation | async-start | bytes 16777216 | tf_op jit(solution)/shard_map/all_to_all | solution.py:32
  355.4 4.7 copy-start.3
  360.1 2.9 copy-start.6
  365.6 4.6 copy-start.4
  682.9 19.8 %copy-start.1 = (f32[64,64]{1,0:T(8,128)S(1)}, f32[64,64]{1,0:T(8,128)}, u32[]{:S(2)}) copy-start(f32[64,64]{1,0:T(8,128)} %param.13) | copy-start | bytes 49156
where the time goes:
time: 717 us; the launch traced here: 703 us
  blocking collectives  187 us (26%)
  waiting for transfers between devices  185 us (26%)
  local copies, waits for them, and re-layouts  146 us (20%)
  matrix products  104 us (15%)
  other arithmetic  72.7 us (10%)
  starting transfers between devices  7.86 us (1%)
    all_to_all x1, blocking collectives, exchange(): lax.all_to_all(data, ('band', 'lev'), split_axis=0, concat_axis=0, tiled=...  187 us
    all_to_all x1, waiting for transfers between devices, exchange(): lax.all_to_all(data, ('band', 'lev'), split_axis=0, concat_axis=0, tiled=...  185 us
    unnamed x26, local copies, waits for them, and re-layouts  38.1 us
    dot_general x1, matrix products, shards(): lax.dot_general(returned.reshape(devices * 2 * slots, levels, lats), tabl...  35.7 us
    rev x1, local copies, waits for them, and re-layouts, shards(): (first - second)[:, :, ::-1]  34.2 us
    rev x1, local copies, waits for them, and re-layouts, shards(): south = arrived[:, :, half:][:, :, ::-1]  34.2 us
    dot_general x1, matrix products, shards(): lax.dot_general(table, rows, (((1,), (1,)), ((), ())), precision=PRECISIO...  33.2 us
    mul x1, other arithmetic, shards(): forced = grid_adjoint * (1.0 + trajectory)  27.3 us
  transfers between devices with their start and end apart: 1, of which 1 were waited for; matrix products, arithmetic and copies ran while one was open for 0% of the time, Pallas kernels for 0%

commit v1 on v0

--- a/solution.py
+++ b/solution.py
@@ -1,6 +1,10 @@
+import functools
+
 import jax
 import jax.numpy as jnp
 from jax import lax
+from jax.experimental import pallas as pl
+from jax.experimental.pallas import tpu as pltpu
 from jax.sharding import PartitionSpec as P
 
 PRECISION = lax.Precision.HIGH
@@ -32,7 +36,7 @@
     return lax.all_to_all(data, ("band", "lev"), split_axis=0, concat_axis=0, tiled=True)
 
 
-def shards(
+def plain_shards(
     grid_adjoint,
     trajectory,
     legendre_north,
@@ -104,6 +108,473 @@
     return spectral.transpose(0, 3, 1, 2), jnp.swapaxes(grid, 0, 1)
 
 
+LANES = 128
+SUB = 8
+PAIR = 2
+PIECES = 8
+NN = (((1,), (0,)), ((), ()))
+NT = (((1,), (1,)), ((), ()))
+
+
+def halves_of(x):
+    high = x.astype(jnp.bfloat16)
+    low = (x - high.astype(jnp.float32)).astype(jnp.bfloat16)
+    return high, low
+
+
+def dot3(a, b, dims):
+    def one(x, y):
+        return lax.dot_general(x, y, dims, preferred_element_type=jnp.float32)
+
+    return one(a[0], b[0]) + (one(a[0], b[1]) + one(a[1], b[0]))
+
+
+def fill_table(p_ref, q_ref, cos_ref, sin_ref, high, low):
+    rows, longitudes = high.shape
+    block = min(64, rows)
+
+    def body(r, carry):
+        at = pl.ds(pl.multiple_of(r * block, block), block)
+        p, q, c, s = p_ref[at, :], q_ref[at, :], cos_ref[at, :], sin_ref[at, :]
+        for i in range(longitudes // LANES):
+            h, l = halves_of(p[:, i : i + 1] * c + q[:, i : i + 1] * s)
+            high[at, i * LANES : (i + 1) * LANES] = h
+            low[at, i * LANES : (i + 1) * LANES] = l
+        return carry
+
+    lax.fori_loop(0, rows // block, body, 0)
+
+
+def forward_kernel(
+    dims,
+    grid_ref, traj_ref, p_ref, q_ref, cos_ref, sin_ref, leg_ref, state_ref,
+    valid_ref, helm_ref, rate_ref, into_ref, outof_ref, back_ref,
+    spec_out, returned,
+    high, low, forced, stage, traj, rows_h, rows_l, sending, arrived, synth, leg, state, spec,
+    grid_sem, traj_sem, send_sem, recv_sem, send2_sem, recv2_sem, leg_sem, state_sem, spec_sem,
+):
+    bands, parts, lats, levels, longitudes, slots, depth, half = dims
+    devices = bands * parts
+    every = parts * levels
+    pairs = levels // PAIR
+    unit = 2 * slots
+    message = PAIR * unit
+    band, lev = lax.axis_index("band"), lax.axis_index("lev")
+    me = band * parts + lev
+    south = band >= bands // 2
+
+    def mesh_id(d):
+        return (d // parts, lax.rem(d, parts))
+
+    barrier = pltpu.get_barrier_semaphore()
+
+    def greet(i, carry):
+        pl.semaphore_signal(
+            barrier, inc=1, device_id=mesh_id(jnp.bitwise_xor(me, i)),
+            device_id_type=pl.DeviceIdType.MESH,
+        )
+        return carry
+
+    lax.fori_loop(1, devices, greet, 0)
+
+    span = lats // PIECES
+    count = (levels // SUB) * PIECES
+
+    def load_copies(piece):
+        block, part = piece // PIECES, lax.rem(piece, PIECES)
+        lat = pl.ds(pl.multiple_of(part * span, span), span)
+        cut = pl.ds(pl.multiple_of(block * SUB, SUB), SUB)
+        slot = lax.rem(piece, 2)
+        return (
+            pltpu.make_async_copy(grid_ref.at[lat, cut, :], stage.at[slot], grid_sem.at[slot]),
+            pltpu.make_async_copy(traj_ref.at[lat, cut, :], traj.at[slot], traj_sem.at[slot]),
+        )
+
+    def load_piece(piece):
+        for copy in load_copies(piece):
+            copy.start()
+
+    def finish_piece(piece):
+        block, part = piece // PIECES, lax.rem(piece, PIECES)
+        slot = lax.rem(piece, 2)
+        for copy in load_copies(piece):
+            copy.wait()
+
+        def body(i, carry):
+            at = part * span + i
+            lat = jnp.where(south, lats - 1 - at, at)
+            to = pl.ds(pl.multiple_of((block * lats + lat) * SUB, SUB), SUB)
+            x = stage[slot, i] * (1.0 + traj[slot, i])
+            for j in range(longitudes // LANES):
+                forced[j, to, :] = x[:, j * LANES : (j + 1) * LANES]
+            return carry
+
+        lax.fori_loop(0, span, body, 0)
+
+        @pl.when(piece + 2 < count)
+        def _():
+            load_piece(piece + 2)
+
+    load_piece(jnp.int32(0))
+    load_piece(jnp.int32(1))
+
+    def leg_copy(s, slot):
+        return pltpu.make_async_copy(leg_ref.at[s], leg.at[slot], leg_sem.at[slot])
+
+    def state_copy(s, slot):
+        return pltpu.make_async_copy(state_ref.at[s], state.at[slot], state_sem.at[slot])
+
+    fill_table(p_ref, q_ref, cos_ref, sin_ref, high, low)
+    tall = min(256, devices * unit)
+
+    def send_copy(q, d):
+        return pltpu.make_async_remote_copy(
+            src_ref=sending.at[pl.ds(pl.multiple_of((q * devices + d) * message, SUB), message), :],
+            dst_ref=arrived.at[pl.ds(pl.multiple_of((me * pairs + q) * message, SUB), message), :],
+            send_sem=send_sem,
+            recv_sem=recv_sem,
+            device_id=mesh_id(d),
+            device_id_type=pl.DeviceIdType.MESH,
+        )
+
+    def transform(q):
+        first = q * PAIR
+        block, local = first // SUB, lax.rem(first, SUB)
+        for h in range(PAIR):
+            for i in range(longitudes // LANES):
+                x = forced[i, pl.ds(block * lats * SUB + local + h, lats, stride=SUB), :]
+                rh, rl = halves_of(x)
+                rows_h[h * lats : (h + 1) * lats, i * LANES : (i + 1) * LANES] = rh
+                rows_l[h * lats : (h + 1) * lats, i * LANES : (i + 1) * LANES] = rl
+
+        def body(r, carry):
+            at = pl.ds(pl.multiple_of(r * tall, tall), tall)
+            got = dot3((high[at, :], low[at, :]), (rows_h[...], rows_l[...]), NT)
+            first = (q * devices + r * (tall // unit)) * message
+            for d in range(tall // unit):
+                for h in range(PAIR):
+                    to = pl.multiple_of(first + (d * PAIR + h) * unit, SUB)
+                    sending[pl.ds(to, unit), :] = got[
+                        d * unit : (d + 1) * unit, h * lats : (h + 1) * lats
+                    ]
+            return carry
+
+        lax.fori_loop(0, devices * unit // tall, body, 0)
+
+    def send_pair(q):
+        def body(i, carry):
+            send_copy(q, jnp.bitwise_xor(me, devices - 1 - i)).start()
+            return carry
+
+        lax.fori_loop(0, devices - 1, body, 0)
+        pltpu.make_async_copy(
+            sending.at[pl.ds(pl.multiple_of((q * devices + me) * message, SUB), message), :],
+            arrived.at[pl.ds(pl.multiple_of((me * pairs + q) * message, SUB), message), :],
+            recv_sem,
+        ).start()
+
+    per = SUB // PAIR
+
+    def outer(block, carry):
+        def finish(i, c):
+            finish_piece(block * PIECES + i)
+            return c
+
+        lax.fori_loop(0, PIECES, finish, 0)
+
+        def run(j, c):
+            q = block * per + j
+            transform(q)
+
+            @pl.when(q == 0)
+            def _():
+                pl.semaphore_wait(barrier, devices - 1)
+
+            send_pair(q)
+            return c
+
+        lax.fori_loop(0, per, run, 0)
+        return carry
+
+    lax.fori_loop(0, levels // SUB, outer, 0)
+
+    leg_copy(0, 0).start()
+    state_copy(0, 0).start()
+    pltpu.make_async_copy(arrived, arrived, recv_sem).wait()
+
+    lane = lax.broadcasted_iota(jnp.int32, (2 * every, depth), 1)
+    even = lax.rem(lane, 2) == 0
+    folds = bands // 2
+
+    def column(b, s):
+        return jnp.concatenate(
+            [
+                arrived[pl.ds(b * every * unit + 2 * s + c, every, stride=unit), :]
+                for c in range(2)
+            ],
+            axis=0,
+        )
+
+    def send2_copy(s, d):
+        return pltpu.make_async_remote_copy(
+            src_ref=synth.at[pl.ds(pl.multiple_of((s * devices + d) * 2 * levels, SUB), 2 * levels), :],
+            dst_ref=returned.at[pl.ds(pl.multiple_of((me * slots + s) * 2 * levels, SUB), 2 * levels), :],
+            send_sem=send2_sem,
+            recv_sem=recv2_sem,
+            device_id=mesh_id(d),
+            device_id_type=pl.DeviceIdType.MESH,
+        )
+
+    def one_slot(s, carry):
+        slot = lax.rem(s, 2)
+
+        @pl.when(s + 1 < slots)
+        def _():
+            leg_copy(s + 1, 1 - slot).start()
+            state_copy(s + 1, 1 - slot).start()
+
+        leg_copy(s, slot).wait()
+        state_copy(s, slot).wait()
+        functions = halves_of(leg[slot])
+        evens, odds = [], []
+        for b in range(folds):
+            n, o = column(b, s), column(bands - 1 - b, s)
+            evens.append(n + o)
+            odds.append(n - o)
+        folded = jnp.concatenate(
+            [jnp.concatenate(evens, axis=1), jnp.concatenate(odds, axis=1)], axis=0
+        )
+        both = dot3(halves_of(folded), functions, NT)
+        analysed = jnp.where(even, both[: 2 * every], both[2 * every :])
+        row = pl.ds(s, 1)
+        total = (analysed + state[slot]) * valid_ref[row, :]
+        modes = dot3(halves_of(into_ref[...]), halves_of(total), NN)
+        scaled = modes / (1.0 + helm_ref[row, :] * rate_ref[:, 0:1])
+        scaled = halves_of(scaled)
+
+        @pl.when(s >= 2)
+        def _():
+            pltpu.make_async_copy(spec.at[slot], spec_out.at[s - 2], spec_sem.at[slot]).wait()
+
+        spec[slot] = dot3(halves_of(outof_ref[...]), scaled, NN)
+        pltpu.make_async_copy(spec.at[slot], spec_out.at[s], spec_sem.at[slot]).start()
+        coeffs = dot3(halves_of(back_ref[...]), scaled, NN)
+        split = jnp.concatenate(
+            [jnp.where(even, coeffs, 0.0), jnp.where(even, 0.0, coeffs)], axis=0
+        )
+        parts_of = dot3(halves_of(split), functions, NN)
+        first, second = parts_of[: 2 * every], parts_of[2 * every :]
+        north, other = first + second, first - second
+        base = s * devices * 2 * levels
+        for b in range(folds):
+            cut = slice(b * LANES, (b + 1) * LANES)
+            to = pl.multiple_of(base + b * 2 * every, SUB)
+            synth[pl.ds(to, 2 * every), :] = north[:, cut]
+            to = pl.multiple_of(base + (bands - 1 - b) * 2 * every, SUB)
+            synth[pl.ds(to, 2 * every), :] = other[:, cut]
+
+        def body(i, c):
+            send2_copy(s, jnp.bitwise_xor(me, devices - 1 - i)).start()
+            return c
+
+        lax.fori_loop(0, devices - 1, body, 0)
+        pltpu.make_async_copy(
+            synth.at[pl.ds(pl.multiple_of((s * devices + me) * 2 * levels, SUB), 2 * levels), :],
+            returned.at[pl.ds(pl.multiple_of((me * slots + s) * 2 * levels, SUB), 2 * levels), :],
+            recv2_sem,
+        ).start()
+        return carry
+
+    lax.fori_loop(0, slots, one_slot, 0)
+    for s in range(max(slots - 2, 0), slots):
+        pltpu.make_async_copy(spec.at[s % 2], spec_out.at[s], spec_sem.at[s % 2]).wait()
+    sent = pl.ds(0, pairs * (devices - 1) * message)
+    pltpu.make_async_copy(sending.at[sent, :], sending.at[sent, :], send_sem).wait()
+    sent = pl.ds(0, slots * (devices - 1) * 2 * levels)
+    pltpu.make_async_copy(synth.at[sent, :], synth.at[sent, :], send2_sem).wait()
+    pltpu.make_async_copy(returned, returned, recv2_sem).wait()
+
+
+def inverse_kernel(
+    dims, returned, p_ref, q_ref, cos_ref, sin_ref, grid_out,
+    high, low, arrived, turned, rows_h, rows_l, result, in_sem, out_sem,
+):
+    bands, parts, lats, levels, longitudes, slots, depth, half = dims
+    south = lax.axis_index("band") >= bands // 2
+    waves = bands * parts * slots * 2
+    step = waves // PIECES
+    blocks = step // LANES
+
+    def load(i):
+        at = pl.ds(pl.multiple_of(i * step * levels, SUB), step * levels)
+        return pltpu.make_async_copy(returned.at[at, :], arrived.at[at, :], in_sem.at[i])
+
+    for i in range(PIECES):
+        load(i).start()
+    fill_table(p_ref, q_ref, cos_ref, sin_ref, high, low)
+    for i in range(PIECES):
+        load(i).wait()
+
+        def pull(l, carry):
+            x = arrived[pl.ds(i * step * levels + l, step, stride=levels), :].T
+            for j in range(blocks):
+                turned[i * blocks + j, pl.ds(l, lats, stride=levels), :] = x[
+                    :, j * LANES : (j + 1) * LANES
+                ]
+            return carry
+
+        lax.fori_loop(0, levels, pull, 0)
+
+        def split(r, carry):
+            lat = jnp.where(south, lats - 1 - r, r)
+            at = pl.ds(pl.multiple_of(lat * levels, levels), levels)
+            to = pl.ds(pl.multiple_of(r * levels, levels), levels)
+            for j in range(blocks):
+                k = i * blocks + j
+                h, l = halves_of(turned[k, at, :])
+                rows_h[to, k * LANES : (k + 1) * LANES] = h
+                rows_l[to, k * LANES : (k + 1) * LANES] = l
+            return carry
+
+        lax.fori_loop(0, lats, split, 0)
+    wide = 256
+    span = lats // PIECES
+
+    def out_copy(block, slot):
+        return pltpu.make_async_copy(
+            result.at[slot],
+            grid_out.at[pl.ds(pl.multiple_of(block * span, span), span), :, :],
+            out_sem.at[slot],
+        )
+
+    def outer(block, carry):
+        slot = lax.rem(block, 2)
+
+        @pl.when(block >= 2)
+        def _():
+            out_copy(block - 2, slot).wait()
+
+        at = pl.ds(pl.multiple_of(block * span * levels, levels), span * levels)
+
+        def inner(w, c):
+            to = pl.ds(pl.multiple_of(w * wide, wide), wide)
+            got = dot3((rows_h[at, :], rows_l[at, :]), (high[:, to], low[:, to]), NN)
+            result[slot, :, :, to] = got.reshape(span, levels, wide)
+            return c
+
+        lax.fori_loop(0, longitudes // wide, inner, 0)
+        out_copy(block, slot).start()
+        return carry
+
+    lax.fori_loop(0, PIECES, outer, 0)
+    for block in range(PIECES - 2, PIECES):
+        out_copy(block, block % 2).wait()
+
+
+def shards(
+    grid_adjoint, trajectory, legendre_north, slot_wavenumber, spectral_state,
+    to_modes, from_modes, rates,
+):
+    lats, levels, longitudes = grid_adjoint.shape
+    slots, depth, half = legendre_north.shape
+    bands = lax.axis_size("band")
+    parts = lax.axis_size("lev")
+    devices = bands * parts
+    every = parts * levels
+    fits = (
+        lats == LANES and levels % SUB == 0 and longitudes % (2 * LANES) == 0
+        and bands % 2 == 0 and half == bands // 2 * lats and depth % LANES == 0
+        and (2 * slots) % SUB == 0 and every == to_modes.shape[0]
+        and devices & (devices - 1) == 0 and (devices * 2 * slots) % 256 == 0
+    )
+    if not fits:
+        return plain_shards(
+            grid_adjoint, trajectory, legendre_north, slot_wavenumber, spectral_state,
+            to_modes, from_modes, rates,
+        )
+    dims = (bands, parts, lats, levels, longitudes, slots, depth, half)
+    me = lax.axis_index("band") * parts + lax.axis_index("lev")
+    own = lax.dynamic_slice_in_dim(slot_wavenumber, me * slots, slots)
+
+    scale = jnp.float32(longitudes) ** (-0.5)
+    coarse = longitudes // LANES
+    cos_a, sin_a = angle_parts(jnp.arange(coarse, dtype=jnp.int32) * LANES, slot_wavenumber, longitudes)
+    cos_b, sin_b = angle_parts(jnp.arange(LANES, dtype=jnp.int32), slot_wavenumber, longitudes)
+    cos_a, sin_a = cos_a * scale, sin_a * scale
+    waves = devices * slots * 2
+    p = jnp.stack([cos_a, -sin_a], axis=1).reshape(waves, coarse)
+    q = jnp.stack([-sin_a, -cos_a], axis=1).reshape(waves, coarse)
+    cos_b = jnp.repeat(cos_b, 2, axis=0)
+    sin_b = jnp.repeat(sin_b, 2, axis=0)
+
+    depth_index = jnp.arange(depth, dtype=jnp.int32)
+    valid = (depth_index[None, :] < depth - own[:, None]).astype(jnp.float32)
+    degree = (own[:, None] + depth_index[None, :]).astype(jnp.float32)
+    helm = degree * (degree + 1.0) / (depth * (depth - 1.0))
+    rate = jnp.broadcast_to(jnp.tile(rates, 2)[:, None], (2 * every, LANES))
+
+    eye = jnp.eye(2, dtype=jnp.float32)
+    natural = (eye[:, None, :, None] * to_modes[None, :, None, :]).reshape(2 * every, 2 * every)
+    outof = (eye[:, None, :, None] * from_modes[None, :, None, :]).reshape(2 * every, 2 * every)
+    back = outof.reshape(2, parts, levels, 2 * every).transpose(1, 0, 2, 3).reshape(2 * every, 2 * every)
+    hbm = pl.BlockSpec(memory_space=pl.ANY)
+    vmem = pl.BlockSpec(memory_space=pltpu.VMEM)
+    f32, bf16 = jnp.float32, jnp.bfloat16
+    dma = pltpu.SemaphoreType.DMA
+    state = spectral_state.transpose(0, 2, 3, 1).reshape(slots, 2 * every, depth)
+    spectral, returned = pl.pallas_call(
+        functools.partial(forward_kernel, dims),
+        out_shape=(
+            jax.ShapeDtypeStruct((slots, 2 * every, depth), f32),
+            jax.ShapeDtypeStruct((waves * levels, lats), f32),
+        ),
+        in_specs=[hbm, hbm] + [vmem] * 4 + [hbm, hbm] + [vmem] * 6,
+        out_specs=(hbm, hbm),
+        scratch_shapes=[
+            pltpu.VMEM((waves, longitudes), bf16),
+            pltpu.VMEM((waves, longitudes), bf16),
+            pltpu.VMEM((longitudes // LANES, levels * lats, LANES), f32),
+            pltpu.VMEM((2, lats // PIECES, SUB, longitudes), f32),
+            pltpu.VMEM((2, lats // PIECES, SUB, longitudes), f32),
+            pltpu.VMEM((PAIR * lats, longitudes), bf16),
+            pltpu.VMEM((PAIR * lats, longitudes), bf16),
+            pltpu.VMEM((levels * waves, lats), f32),
+            pltpu.VMEM((levels * waves, lats), f32),
+            pltpu.VMEM((waves * levels, lats), f32),
+            pltpu.VMEM((2, depth, half), f32),
+            pltpu.VMEM((2, 2 * every, depth), f32),
+            pltpu.VMEM((2, 2 * every, depth), f32),
+            dma((2,)), dma((2,)), dma, dma, dma, dma, dma((2,)), dma((2,)), dma((2,)),
+        ],
+        compiler_params=pltpu.CompilerParams(
+            collective_id=0, has_side_effects=True, vmem_limit_bytes=67_043_328
+        ),
+        name="spectral",
+    )(
+        grid_adjoint, trajectory, p, q, cos_b, sin_b, legendre_north, state,
+        valid, helm, rate, natural, outof, back,
+    )
+    grid = pl.pallas_call(
+        functools.partial(inverse_kernel, dims),
+        out_shape=jax.ShapeDtypeStruct(grid_adjoint.shape, f32),
+        in_specs=[hbm] + [vmem] * 4,
+        out_specs=hbm,
+        scratch_shapes=[
+            pltpu.VMEM((waves, longitudes), bf16),
+            pltpu.VMEM((waves, longitudes), bf16),
+            pltpu.VMEM((waves * levels, lats), f32),
+            pltpu.VMEM((waves // LANES, lats * levels, LANES), f32),
+            pltpu.VMEM((levels * lats, waves), bf16),
+            pltpu.VMEM((levels * lats, waves), bf16),
+            pltpu.VMEM((2, lats // PIECES, levels, longitudes), f32),
+            dma((PIECES,)), dma((2,)),
+        ],
+        compiler_params=pltpu.CompilerParams(vmem_limit_bytes=67_043_328),
+        name="synthesis",
+    )(returned, p, q, cos_b, sin_b)
+    return spectral.reshape(slots, 2, every, depth).transpose(0, 3, 1, 2), grid
+
+
 def solution(mesh):
     return jax.shard_map(
         shards,

time: 717 us -> 476 us (0.66); the launches traced: 703 us -> 476 us
  Pallas kernels: 0 us -> 456 us
  blocking collectives: 187 us -> 0 us
  waiting for transfers between devices: 185 us -> 0 us
  local copies, waits for them, and re-layouts: 146 us -> 12.9 us
  matrix products: 104 us -> 0 us
  other arithmetic: 72.7 us -> 6.35 us
  starting transfers between devices: 7.86 us -> 0 us
    pallas_call x0 -> x2, Pallas kernels: none -> 456 us  [the longest x1 387 us: shards(): pl.pallas_call(functools.partial(forward_kernel, dims), out_shape=(jax.Sh...]
    all_to_all x1 -> x0, blocking collectives: 187 us -> none  [exchange(): lax.all_to_all(data, ('band', 'lev'), split_axis=0, concat_axis=0, tiled=...]
    all_to_all x1 -> x0, waiting for transfers between devices: 185 us -> none  [exchange(): lax.all_to_all(data, ('band', 'lev'), split_axis=0, concat_axis=0, tiled=...]
    dot_general x6 -> x0, matrix products: 104 us -> none  [the longest x1 35.7 us: shards(): lax.dot_general(returned.reshape(devices * 2 * slots, levels, lats), tabl...]
    rev x2 -> x0, local copies, waits for them, and re-layouts: 68.4 us -> none  [the longest x1 34.2 us: shards(): (first - second)[:, :, ::-1]]
    unnamed x26 -> x1, local copies, waits for them, and re-layouts: 38.1 us -> 4.91 us
    reshape x3 -> x0, local copies, waits for them, and re-layouts: 26.7 us -> none  [the longest x1 9.25 us: shards(): returned = exchange(whole.reshape(devices, 2 * slots, levels * lats))]
    mul x3, other arithmetic: 28.2 us -> 1.55 us  [the longest x2 1.55 us: shards(): eye[:, None, :, None] * from_modes[None, :, None, :]]
  transfers between devices with their start and end apart: 1 -> 0, of which waited for: 1 -> 0; matrix products, arithmetic and copies ran while one was open for 0% -> 0% of each run, Pallas kernels for 0% -> 0%
where the time goes in v1:
time: 476 us
  Pallas kernels  456 us (96%)
  local copies, waits for them, and re-layouts  12.9 us (3%)
  other arithmetic  6.35 us (1%)
    pallas_call x1, Pallas kernels, shards(): pl.pallas_call(functools.partial(forward_kernel, dims), out_shape=(jax.Sh...  387 us
    pallas_call x1, Pallas kernels, shards(): pl.pallas_call(functools.partial(inverse_kernel, dims), out_shape=jax.Sha...  68.9 us

profile of v1, /device:TPU:0, one launch (start us, length us, event | category | flops | bytes accessed | tf_op | source)
XLA Modules:
  0.0 475.7 jit_solution(8357969926079369717)
XLA Ops:
  0.6 0.8 broadcast_subtract_fusion
  1.4 0.7 tile.2
  2.1 0.1 broadcast_in_dim.10
  2.2 0.1 mul.190
  2.2 0.1 mul.191
  2.3 0.7 fusion.12.valid_ref
  3.0 0.7 fusion.10.helm_ref
  3.7 0.7 broadcast_in_dim.11.rate_ref
  4.4 0.8 mul.193
  5.2 0.1 mul.194
  5.3 0.6 broadcast_multiply_fusion.2
  5.9 0.9 fusion.13
  6.8 0.9 broadcast_multiply_fusion
  7.7 0.8 mul.189.outof_ref
  8.5 0.8 mul.186.into_ref
  9.2 1.0 copy.11
  10.3 1.0 copy.10
  11.3 1.8 fusion.6
  13.0 1.0 broadcast_in_dim.9
  14.0 1.0 broadcast_in_dim.8
  15.0 386.9 %spectral.1 = (f32[16,128,512]{2,1,0:T(8,128)}, f32[16384,128]{1,0:T(8,128)}) custom-call(f32[128,16,2048]{2,1,0:T(8,128)} %grid_ref.1, f32[128,16,2048]{2,1,0:T(8,128)} %traj_ref.1, f32[1024,16]{1,0:T(8,128)} %bitcast.13, f32[1024,16]{1,0:T(8,128)} %bitcast.11, f32[1024,128]{1,0:T(8,128)} %bitcast.17, f32[1024,128]{1,0:T(8,128)} %bitcast.15, ...), custom_call_target="tpu_custom_call" | custom-call | tf_op jit(solution)/shard_map/spectral/pallas_call | solution.py:525
  401.9 68.9 %synthesis.1 = f32[128,16,2048]{2,1,0:T(8,128)} custom-call(f32[16384,128]{1,0:T(8,128)} %get-tuple-element.5.returned, f32[1024,16]{1,0:T(8,128)} %bitcast.14, f32[1024,16]{1,0:T(8,128)} %bitcast.12, f32[1024,128]{1,0:T(8,128)} %bitcast.18, f32[1024,128]{1,0:T(8,128)} %bitcast.16), custom_call_target="tpu_custom_call" | custom-call | tf_op jit(solution)/shard_map/synthesis/pallas_call | solution.py:557
  470.8 4.9 %copy.13 = f32[16,512,2,64]{1,3,2,0:T(8,128)} copy(f32[16,512,2,64]{1,3,2,0:T(8,128)} %bitcast.19) | data formatting | bytes 8388608
  (3 shorter events, 0.0 us)

commit v2 on v1

v2 whole, which is shorter than its diff:
```python
import functools
import math

import jax
import jax.numpy as jnp
from jax import lax
from jax.experimental import pallas as pl
from jax.experimental.pallas import tpu as pltpu
from jax.sharding import PartitionSpec as P

PRECISION = lax.Precision.HIGH


def angle_parts(steps, waves, longitudes):
    phase = waves[:, None] * steps[None, :] % longitudes
    angles = phase.astype(jnp.float32) * (2.0 * jnp.pi / longitudes)
    return jnp.cos(angles), jnp.sin(angles)


def wave_rows(longitudes, waves, devices):
    fine = min(128, longitudes)
    coarse = longitudes // fine
    scale = jnp.float32(longitudes) ** (-0.5)
    cos_a, sin_a = angle_parts(jnp.arange(coarse, dtype=jnp.int32) * fine, waves, longitudes)
    cos_b, sin_b = angle_parts(jnp.arange(fine, dtype=jnp.int32), waves, longitudes)
    cos_a, sin_a, cos_b, sin_b = lax.optimization_barrier(
        (cos_a * scale, sin_a * scale, cos_b, sin_b)
    )
    cos_at = [cos_a[:, i : i + 1] * cos_b - sin_a[:, i : i + 1] * sin_b for i in range(coarse)]
    sin_at = [-sin_a[:, i : i + 1] * cos_b - cos_a[:, i : i + 1] * sin_b for i in range(coarse)]
    cosine = jnp.concatenate(cos_at, axis=1).reshape(devices, -1, longitudes)
    negsine = jnp.concatenate(sin_at, axis=1).reshape(devices, -1, longitudes)
    return jnp.stack([cosine, negsine], axis=1).reshape(-1, longitudes)


def exchange(data):
    return lax.all_to_all(data, ("band", "lev"), split_axis=0, concat_axis=0, tiled=True)


def plain_shards(
    grid_adjoint,
    trajectory,
    legendre_north,
    slot_wavenumber,
    spectral_state,
    to_modes,
    from_modes,
    rates,
):
    lats, levels, longitudes = grid_adjoint.shape
    slots, depth, half = legendre_north.shape
    bands = lax.axis_size("band")
    parts = lax.axis_size("lev")
    devices = bands * parts
    every = parts * levels
    me = lax.axis_index("band") * parts + lax.axis_index("lev")
    own_waves = lax.dynamic_slice_in_dim(slot_wavenumber, me * slots, slots)
    table = wave_rows(longitudes, slot_wavenumber, devices)
    even_k = jnp.arange(depth, dtype=jnp.int32) % 2 == 0

    forced = grid_adjoint * (1.0 + trajectory)
    rows = jnp.swapaxes(forced, 0, 1).reshape(levels * lats, longitudes)
    fourier = lax.dot_general(
        table, rows, (((1,), (1,)), ((), ())), precision=PRECISION, preferred_element_type=jnp.float32
    )
    arrived = exchange(fourier.reshape(devices, 2 * slots, levels * lats))
    arrived = arrived.reshape(bands, parts, 2, slots, levels, lats)
    arrived = arrived.transpose(3, 2, 1, 4, 0, 5).reshape(slots, 2 * every, bands * lats)
    north = arrived[:, :, :half]
    south = arrived[:, :, half:][:, :, ::-1]
    folded = jnp.concatenate([north + south, north - south], axis=1)
    both = lax.dot_general(
        folded, legendre_north, (((2,), (2,)), ((0,), (0,))), precision=PRECISION,
        preferred_element_type=jnp.float32,
    )
    analysed = jnp.where(even_k, both[:, : 2 * every], both[:, 2 * every :])
    analysed = analysed.reshape(slots, 2, every, depth)

    state = spectral_state.transpose(0, 2, 3, 1)
    depth_index = jnp.arange(depth, dtype=jnp.int32)
    valid = (depth_index[None, :] < depth - own_waves[:, None]).astype(jnp.float32)
    total = (analysed + state) * valid[:, None, None, :]
    degree = (own_waves[:, None] + depth_index[None, :]).astype(jnp.float32)
    helm = degree * (degree + 1.0) / (depth * (depth - 1.0))
    modes = jnp.einsum("sclk,pl->scpk", total, to_modes, precision=PRECISION)
    scaled = modes / (1.0 + helm[:, None, None, :] * rates[None, None, :, None])
    spectral = jnp.einsum("scpk,lp->sclk", scaled, from_modes, precision=PRECISION)

    coeffs = spectral.reshape(slots, 2 * every, depth)
    split = jnp.concatenate(
        [jnp.where(even_k, coeffs, 0.0), jnp.where(even_k, 0.0, coeffs)], axis=1
    )
    halves = lax.dot_general(
        split, legendre_north, (((2,), (1,)), ((0,), (0,))), precision=PRECISION,
        preferred_element_type=jnp.float32,
    )
    first = halves[:, : 2 * every]
    second = halves[:, 2 * every :]
    whole = jnp.concatenate([first + second, (first - second)[:, :, ::-1]], axis=2)
    whole = whole.reshape(slots, 2, parts, levels, bands, lats).transpose(4, 2, 1, 0, 3, 5)
    returned = exchange(whole.reshape(devices, 2 * slots, levels * lats))
    grid = lax.dot_general(
        returned.reshape(devices * 2 * slots, levels, lats),
        table,
        (((0,), (0,)), ((), ())),
        precision=PRECISION,
        preferred_element_type=jnp.float32,
    )
    return spectral.transpose(0, 3, 1, 2), jnp.swapaxes(grid, 0, 1)


LANES = 128
SUB = 8
PAIR = 2
PIECES = 8
GROUP = 4
NN = (((1,), (0,)), ((), ()))
NT = (((1,), (1,)), ((), ()))


def halves_of(x):
    high = x.astype(jnp.bfloat16)
    low = (x - high.astype(jnp.float32)).astype(jnp.bfloat16)
    return high, low


def dot1(x, y, dims):
    return lax.dot_general(x, y, dims, preferred_element_type=jnp.float32)


def dot3(a, b, dims):
    return dot1(a[0], b[0], dims) + (dot1(a[0], b[1], dims) + dot1(a[1], b[0], dims))


def aligned(start, size):
    return pl.ds(pl.multiple_of(start, size & -size), size)


def circle(phase, longitudes):
    quarter = longitudes // 4
    quadrant = phase // quarter
    rest = phase - quadrant * quarter
    flip = rest > quarter // 2
    angle = jnp.where(flip, quarter - rest, rest).astype(jnp.float32) * (
        2.0 * math.pi / longitudes
    )
    z = angle * angle
    sine = angle * (
        1.0 + z * (-1 / 6 + z * (1 / 120 + z * (-1 / 5040 + z * (1 / 362880))))
    )
    cosine = 1.0 + z * (
        -0.5 + z * (1 / 24 + z * (-1 / 720 + z * (1 / 40320 + z * (-1 / 3628800))))
    )
    c, s = jnp.where(flip, sine, cosine), jnp.where(flip, cosine, sine)
    odd = lax.rem(quadrant, 2) == 1
    c, s = jnp.where(odd, s, c), jnp.where(odd, c, s)
    c = jnp.where((quadrant == 1) | (quadrant == 2), -c, c)
    return c, jnp.where(quadrant >= 2, -s, s)


def table_rows(waves, imaginary, longitudes):
    column = lax.broadcasted_iota(jnp.int32, waves.shape, 1)
    ca, sa = circle(lax.rem(waves * (column * LANES), longitudes), longitudes)
    cb, sb = circle(lax.rem(waves * column, longitudes), longitudes)
    scale = float(longitudes) ** -0.5
    ca, sa = ca * scale, sa * scale
    p = jnp.where(imaginary, -sa, ca)
    q = jnp.where(imaginary, -ca, -sa)
    return [
        halves_of(p[:, i : i + 1] * cb + q[:, i : i + 1] * sb)
        for i in range(longitudes // LANES)
    ]


def forward_kernel(
    dims,
    grid_ref, traj_ref, wave_ref, leg_ref, state_ref, rate_ref, to_ref, from_ref,
    spec_out, returned, partial,
    high, low, forced, stage, traj, rows_h, rows_l, sending, arrived, synth, leg, state, spec,
    into, outof, back, pulled, turned,
    grid_sem, traj_sem, send_sem, recv_sem, send2_sem, recv2_sem, leg_sem, state_sem, spec_sem,
    pull_sem, part_sem,
):
    bands, parts, lats, levels, longitudes, slots, depth, half = dims
    devices = bands * parts
    every = parts * levels
    pairs = levels // PAIR
    unit = 2 * slots
    message = PAIR * unit
    small = 2 * GROUP
    tall = devices * small
    groups = slots // GROUP
    wide = longitudes // LANES
    band, lev = lax.axis_index("band"), lax.axis_index("lev")
    me = band * parts + lev
    south = band >= bands // 2

    def mesh_id(d):
        return (d // parts, lax.rem(d, parts))

    barrier = pltpu.get_barrier_semaphore()

    def greet(i, carry):
        pl.semaphore_signal(
            barrier, inc=1, device_id=mesh_id(jnp.bitwise_xor(me, i)),
            device_id_type=pl.DeviceIdType.MESH,
        )
        return carry

    lax.fori_loop(1, devices, greet, 0)

    span = lats // PIECES
    count = (levels // SUB) * PIECES

    def load_copies(piece):
        block, part = piece // PIECES, lax.rem(piece, PIECES)
        lat = aligned(part * span, span)
        cut = aligned(block * SUB, SUB)
        slot = lax.rem(piece, 2)
        return (
            pltpu.make_async_copy(grid_ref.at[lat, cut, :], stage.at[slot], grid_sem.at[slot]),
            pltpu.make_async_copy(traj_ref.at[lat, cut, :], traj.at[slot], traj_sem.at[slot]),
        )

    def load_piece(piece):
        for copy in load_copies(piece):
            copy.start()

    def finish_piece(piece):
        block, part = piece // PIECES, lax.rem(piece, PIECES)
        slot = lax.rem(piece, 2)
        for copy in load_copies(piece):
            copy.wait()

        def body(i, carry):
            at = part * span + i
            lat = jnp.where(south, lats - 1 - at, at)
            to = aligned((block * lats + lat) * SUB, SUB)
            x = stage[slot, i] * (1.0 + traj[slot, i])
            for j in range(wide):
                forced[j, to, :] = x[:, j * LANES : (j + 1) * LANES]
            return carry

        lax.fori_loop(0, span, body, 0)

        @pl.when(piece + 2 < count)
        def _():
            load_piece(piece + 2)

    load_piece(jnp.int32(0))
    load_piece(jnp.int32(1))

    def leg_copy(s, slot):
        return pltpu.make_async_copy(leg_ref.at[s], leg.at[slot], leg_sem.at[slot])

    def state_copy(s, slot):
        return pltpu.make_async_copy(state_ref.at[s], state.at[slot], state_sem.at[slot])

    block_rows = 64

    def fill(r, carry):
        at = aligned(r * block_rows, block_rows)
        waves = wave_ref[at, :]
        imaginary = lax.rem(lax.broadcasted_iota(jnp.int32, waves.shape, 0), 2) == 1
        for i, (h, l) in enumerate(table_rows(waves, imaginary, longitudes)):
            high[at, i * LANES : (i + 1) * LANES] = h
            low[at, i * LANES : (i + 1) * LANES] = l
        return carry

    lax.fori_loop(0, devices * unit // block_rows, fill, 0)
    for m in (into, outof, back):
        m[...] = jnp.zeros_like(m)
    for c in range(2):
        cut = slice(c * every, (c + 1) * every)
        into[cut, cut] = to_ref[...]
        outof[cut, cut] = from_ref[...]
        for p in range(parts):
            at = (2 * p + c) * levels
            back[at : at + levels, cut] = from_ref[p * levels : (p + 1) * levels, :]

    def send_copy(q, d):
        return pltpu.make_async_remote_copy(
            src_ref=sending.at[aligned((q * devices + d) * message, message), :],
            dst_ref=arrived.at[aligned((me * pairs + q) * message, message), :],
            send_sem=send_sem,
            recv_sem=recv_sem,
            device_id=mesh_id(d),
            device_id_type=pl.DeviceIdType.MESH,
        )

    def transform(q):
        first = q * PAIR
        block, local = first // SUB, lax.rem(first, SUB)
        for h in range(PAIR):
            for i in range(wide):
                x = forced[i, pl.ds(block * lats * SUB + local + h, lats, stride=SUB), :]
                rh, rl = halves_of(x)
                rows_h[h * lats : (h + 1) * lats, i * LANES : (i + 1) * LANES] = rh
                rows_l[h * lats : (h + 1) * lats, i * LANES : (i + 1) * LANES] = rl

        def body(r, carry):
            at = aligned(r * tall, tall)
            got = dot3((high[at, :], low[at, :]), (rows_h[...], rows_l[...]), NT)
            for d in range(devices):
                for h in range(PAIR):
                    to = (q * devices + d) * message + h * unit + r * small
                    sending[aligned(to, small), :] = got[
                        d * small : (d + 1) * small, h * lats : (h + 1) * lats
                    ]
            return carry

        lax.fori_loop(0, groups, body, 0)

    def send_pair(q):
        def body(i, carry):
            send_copy(q, jnp.bitwise_xor(me, devices - 1 - i)).start()
            return carry

        lax.fori_loop(0, devices - 1, body, 0)
        pltpu.make_async_copy(
            sending.at[aligned((q * devices + me) * message, message), :],
            arrived.at[aligned((me * pairs + q) * message, message), :],
            recv_sem,
        ).start()

    per = SUB // PAIR

    def outer(block, carry):
        def finish(i, c):
            finish_piece(block * PIECES + i)
            return c

        lax.fori_loop(0, PIECES, finish, 0)

        def run(j, c):
            q = block * per + j
            transform(q)

            @pl.when(q == 0)
            def _():
                pl.semaphore_wait(barrier, devices - 1)

            send_pair(q)
            return c

        lax.fori_loop(0, per, run, 0)
        return carry

    lax.fori_loop(0, levels // SUB, outer, 0)

    leg_copy(0, 0).start()
    state_copy(0, 0).start()
    pltpu.make_async_copy(arrived, arrived, recv_sem).wait()

    lane = lax.broadcasted_iota(jnp.int32, (2 * every, depth), 1)
    even = lax.rem(lane, 2) == 0
    folds = bands // 2
    each = 2 * levels

    def column(b, s):
        return jnp.concatenate(
            [
                arrived[pl.ds(b * every * unit + 2 * s + c, every, stride=unit), :]
                for c in range(2)
            ],
            axis=0,
        )

    def send2_copy(s, d, sem):
        return pltpu.make_async_remote_copy(
            src_ref=synth.at[aligned((s * devices + d) * each, each), :],
            dst_ref=returned.at[me, aligned(s * each, each), :],
            send_sem=send2_sem,
            recv_sem=recv2_sem.at[sem],
            device_id=mesh_id(d),
            device_id_type=pl.DeviceIdType.MESH,
        )

    def one_slot(s, carry):
        slot = lax.rem(s, 2)
        sem = jnp.where(s == slots - 1, groups, s // GROUP)

        @pl.when(s + 1 < slots)
        def _():
            leg_copy(s + 1, 1 - slot).start()
            state_copy(s + 1, 1 - slot).start()

        leg_copy(s, slot).wait()
        state_copy(s, slot).wait()
        functions = halves_of(leg[slot])
        evens, odds = [], []
        for b in range(folds):
            n, o = column(b, s), column(bands - 1 - b, s)
            evens.append(n + o)
            odds.append(n - o)
        folded = jnp.concatenate(
            [jnp.concatenate(evens, axis=1), jnp.concatenate(odds, axis=1)], axis=0
        )
        both = dot3(halves_of(folded), functions, NT)
        analysed = jnp.where(even, both[: 2 * every], both[2 * every :])
        wave = wave_ref[
            pl.ds((s // GROUP * devices + me) * small + lax.rem(s, GROUP) * 2, 1), :
        ]
        wave = jnp.concatenate([wave] * (depth // LANES), axis=1)
        order = lax.broadcasted_iota(jnp.int32, (1, depth), 1)
        degree = (wave + order).astype(jnp.float32)
        helm = degree * (degree + 1.0) / (depth * (depth - 1.0))
        total = jnp.where(order < depth - wave, analysed + state[slot], 0.0)
        modes = dot3(halves_of(into[...]), halves_of(total), NN)
        scaled = halves_of(modes / (1.0 + helm * rate_ref[:, 0:1]))

        @pl.when(s >= 2)
        def _():
            pltpu.make_async_copy(spec.at[slot], spec_out.at[s - 2], spec_sem.at[slot]).wait()

        spec[slot] = dot3(halves_of(outof[...]), scaled, NN)
        pltpu.make_async_copy(spec.at[slot], spec_out.at[s], spec_sem.at[slot]).start()
        coeffs = dot3(halves_of(back[...]), scaled, NN)
        split = jnp.concatenate(
            [jnp.where(even, coeffs, 0.0), jnp.where(even, 0.0, coeffs)], axis=0
        )
        both = dot3(halves_of(split), functions, NN)
        first, second = both[: 2 * every], both[2 * every :]
        north, other = first + second, first - second
        base = s * devices * each
        for b in range(folds):
            cut = slice(b * LANES, (b + 1) * LANES)
            synth[aligned(base + b * 2 * every, 2 * every), :] = north[:, cut]
            synth[aligned(base + (bands - 1 - b) * 2 * every, 2 * every), :] = other[:, cut]

        def body(i, c):
            send2_copy(s, jnp.bitwise_xor(me, devices - 1 - i), sem).start()
            return c

        lax.fori_loop(0, devices - 1, body, 0)
        pltpu.make_async_copy(
            synth.at[aligned((s * devices + me) * each, each), :],
            returned.at[me, aligned(s * each, each), :],
            recv2_sem.at[sem],
        ).start()
        return carry

    lax.fori_loop(0, slots, one_slot, 0)

    block = 256

    def part_copy(m):
        at = aligned(m * block, block)
        return pltpu.make_async_copy(forced.at[:, at, :], partial.at[:, at, :], part_sem)

    for g in range(groups):
        last = g == groups - 1
        rows = (GROUP - 1 if last else GROUP) * each
        here = returned.at[:, g * GROUP * each : g * GROUP * each + rows, :]
        into_vmem = pulled.at[:, 0:rows, :]
        pltpu.make_async_copy(here, here, recv2_sem.at[g]).wait()
        copy = pltpu.make_async_copy(here, into_vmem, pull_sem)
        copy.start()
        copy.wait()
        flat = pulled.reshape(devices * GROUP * each, lats)

        def pull(l, carry):
            x = flat[pl.ds(l, tall, stride=levels), :]
            if last:
                row = lax.rem(lax.broadcasted_iota(jnp.int32, x.shape, 0), small)
                x = jnp.where(row < small - 2, x, 0.0)
            x = x.T
            for j in range(tall // LANES):
                turned[j, pl.ds(l, lats, stride=levels), :] = x[:, j * LANES : (j + 1) * LANES]
            return carry

        lax.fori_loop(0, levels, pull, 0)

        def multiply(m, carry):
            for r in range(block // levels):
                to = m * (block // levels) + r
                lat = jnp.where(south, lats - 1 - to, to)
                for j in range(tall // LANES):
                    h, l = halves_of(turned[j, aligned(lat * levels, levels), :])
                    rows_h[r * levels : (r + 1) * levels, j * LANES : (j + 1) * LANES] = h
                    rows_l[r * levels : (r + 1) * levels, j * LANES : (j + 1) * LANES] = l
            ah, al = rows_h[:block, :tall], rows_l[:block, :tall]
            at = aligned(m * block, block)

            def inner(w, c):
                cut = aligned(w * 2 * LANES, 2 * LANES)
                rows_at = slice(g * tall, (g + 1) * tall)
                got = dot3((ah, al), (high[rows_at, cut], low[rows_at, cut]), NN)
                for j in range(2):
                    x = got[:, j * LANES : (j + 1) * LANES]
                    if g > 0:
                        x = x + forced[2 * w + j, at, :]
                    forced[2 * w + j, at, :] = x
                return c

            lax.fori_loop(0, wide // 2, inner, 0)
            if last:
                part_copy(m).start()
            return carry

        lax.fori_loop(0, lats * levels // block, multiply, 0)

    for s in range(max(slots - 2, 0), slots):
        pltpu.make_async_copy(spec.at[s % 2], spec_out.at[s], spec_sem.at[s % 2]).wait()
    pltpu.make_async_copy(forced, partial, part_sem).wait()
    sent = pl.ds(0, pairs * (devices - 1) * message)
    pltpu.make_async_copy(sending.at[sent, :], sending.at[sent, :], send_sem).wait()
    sent = pl.ds(0, slots * (devices - 1) * each)
    pltpu.make_async_copy(synth.at[sent, :], synth.at[sent, :], send2_sem).wait()
    final = returned.at[:, (slots - 1) * each : slots * each, :]
    pltpu.make_async_copy(final, final, recv2_sem.at[groups]).wait()


def finish_kernel(
    dims, returned, partial, spectral, wave_ref, grid_out, spec_out,
    pulled, turned, stacked, table, before, result, spec,
    pull_sem, in_sem, out_sem, spec_in, spec_done,
):
    bands, parts, lats, levels, longitudes, slots, depth, half = dims
    devices = bands * parts
    each = 2 * levels
    small = 2 * GROUP
    wide = longitudes // LANES
    south = lax.axis_index("band") >= bands // 2
    span = lats // PIECES
    block = span * levels

    def in_copy(m, slot):
        at = aligned(m * block, block)
        return pltpu.make_async_copy(partial.at[:, at, :], before.at[slot], in_sem.at[slot])

    def out_copy(m, slot):
        return pltpu.make_async_copy(
            result.at[slot], grid_out.at[aligned(m * span, span), :, :], out_sem.at[slot]
        )

    pull = pltpu.make_async_copy(
        returned.at[:, (slots - 1) * each : slots * each, :], pulled, pull_sem
    )
    pull.start()
    in_copy(0, 0).start()
    in_copy(1, 1).start()
    spec_copy = pltpu.make_async_copy(spectral, spec, spec_in)
    spec_copy.start()

    first = (slots // GROUP - 1) * devices * small + small - 2
    waves = wave_ref[pl.ds(first, devices, stride=small), :]
    waves = jnp.concatenate([waves, waves], axis=0)
    imaginary = lax.broadcasted_iota(jnp.int32, waves.shape, 0) >= devices
    short = 2 * devices
    for i, (h, l) in enumerate(table_rows(waves, imaginary, longitudes)):
        cut = slice(i * LANES, (i + 1) * LANES)
        table[0:short, cut] = h
        table[short : 2 * short, cut] = l
        table[2 * short : 3 * short, cut] = h
        table[3 * short : 4 * short, cut] = jnp.zeros_like(h)
    pull.wait()
    flat = pulled.reshape(devices * each, lats)

    def gather(l, carry):
        x = jnp.concatenate(
            [flat[pl.ds(c * levels + l, devices, stride=each), :] for c in range(2)], axis=0
        )
        turned[pl.ds(l, lats, stride=levels), :] = jnp.concatenate([x, x], axis=0).T
        return carry

    lax.fori_loop(0, levels, gather, 0)
    keep = lax.broadcasted_iota(jnp.int32, (levels, LANES), 1) < short

    def split(r, carry):
        lat = jnp.where(south, lats - 1 - r, r)
        h, l = halves_of(turned[aligned(lat * levels, levels), :])
        to = aligned(r * levels, levels)
        stacked[to, 0:LANES] = h
        stacked[to, LANES : 2 * LANES] = jnp.where(keep, l, jnp.zeros_like(l))
        return carry

    lax.fori_loop(0, lats, split, 0)

    def outer(m, carry):
        slot = lax.rem(m, 2)
        in_copy(m, slot).wait()

        @pl.when(m >= 2)
        def _():
            out_copy(m - 2, slot).wait()

        a = stacked[aligned(m * block, block), :]

        def inner(w, c):
            cut = aligned(w * 2 * LANES, 2 * LANES)
            got = dot1(a, table[:, cut], NN)
            for j in range(2):
                x = got[:, j * LANES : (j + 1) * LANES] + before[slot, 2 * w + j]
                to = aligned((2 * w + j) * LANES, LANES)
                result[slot, :, :, to] = x.reshape(span, levels, LANES)
            return c

        lax.fori_loop(0, wide // 2, inner, 0)
        out_copy(m, slot).start()

        @pl.when(m + 2 < PIECES)
        def _():
            in_copy(m + 2, slot).start()

        return carry

    spec_copy.wait()
    done = pltpu.make_async_copy(spec, spec_out, spec_done)
    done.start()
    lax.fori_loop(0, PIECES, outer, 0)
    for m in range(PIECES - 2, PIECES):
        out_copy(m, m % 2).wait()
    done.wait()


def shards(
    grid_adjoint, trajectory, legendre_north, slot_wavenumber, spectral_state,
    to_modes, from_modes, rates,
):
    lats, levels, longitudes = grid_adjoint.shape
    slots, depth, half = legendre_north.shape
    bands = lax.axis_size("band")
    parts = lax.axis_size("lev")
    devices = bands * parts
    every = parts * levels
    fits = (
        lats == LANES and levels == 2 * SUB and 4 * devices == LANES
        and longitudes % (2 * LANES) == 0 and longitudes & (longitudes - 1) == 0
        and bands % 2 == 0 and half == bands // 2 * lats and depth % LANES == 0
        and slots % GROUP == 0 and 2 * every == LANES and to_modes.shape[0] == every
    )
    if not fits:
        return plain_shards(
            grid_adjoint, trajectory, legendre_north, slot_wavenumber, spectral_state,
            to_modes, from_modes, rates,
        )
    dims = (bands, parts, lats, levels, longitudes, slots, depth, half)
    count = devices * slots * 2
    waves = slot_wavenumber.reshape(devices, slots // GROUP, GROUP).transpose(1, 0, 2)
    waves = jnp.broadcast_to(waves[:, :, :, None, None], waves.shape + (2, LANES))
    waves = waves.reshape(count, LANES)
    rate = jnp.broadcast_to(rates[None, :, None], (2, every, LANES)).reshape(2 * every, LANES)

    hbm = pl.BlockSpec(memory_space=pl.ANY)
    vmem = pl.BlockSpec(memory_space=pltpu.VMEM)
    f32, bf16 = jnp.float32, jnp.bfloat16
    dma = pltpu.SemaphoreType.DMA
    wide = longitudes // LANES
    state = spectral_state.transpose(0, 2, 3, 1).reshape(slots, 2 * every, depth)
    square = pltpu.VMEM((2 * every, 2 * every), f32)
    spectral, returned, partial = pl.pallas_call(
        functools.partial(forward_kernel, dims),
        out_shape=(
            jax.ShapeDtypeStruct((slots, 2 * every, depth), f32),
            jax.ShapeDtypeStruct((devices, slots * 2 * levels, lats), f32),
            jax.ShapeDtypeStruct((wide, lats * levels, LANES), f32),
        ),
        in_specs=[hbm, hbm, vmem, hbm, hbm, vmem, vmem, vmem],
        out_specs=(hbm, hbm, hbm),
        scratch_shapes=[
            pltpu.VMEM((count, longitudes), bf16),
            pltpu.VMEM((count, longitudes), bf16),
            pltpu.VMEM((wide, levels * lats, LANES), f32),
            pltpu.VMEM((2, lats // PIECES, SUB, longitudes), f32),
            pltpu.VMEM((2, lats // PIECES, SUB, longitudes), f32),
            pltpu.VMEM((PAIR * lats, longitudes), bf16),
            pltpu.VMEM((PAIR * lats, longitudes), bf16),
            pltpu.VMEM((levels * count, lats), f32),
            pltpu.VMEM((levels * count, lats), f32),
            pltpu.VMEM((count * levels, lats), f32),
            pltpu.VMEM((2, depth, half), f32),
            pltpu.VMEM((2, 2 * every, depth), f32),
            pltpu.VMEM((2, 2 * every, depth), f32),
            square, square, square,
            pltpu.VMEM((devices, GROUP * 2 * levels, lats), f32),
            pltpu.VMEM((devices * 2 * GROUP // LANES, lats * levels, LANES), f32),
            dma((2,)), dma((2,)), dma, dma, dma, dma((slots // GROUP + 1,)),
            dma((2,)), dma((2,)), dma((2,)), dma, dma,
        ],
        compiler_params=pltpu.CompilerParams(
            collective_id=0, has_side_effects=True, vmem_limit_bytes=67_043_328
        ),
        name="spectral",
    )(
        grid_adjoint, trajectory, waves, legendre_north, state, rate, to_modes, from_modes,
    )
    grid, spectral = pl.pallas_call(
        functools.partial(finish_kernel, dims),
        out_shape=(
            jax.ShapeDtypeStruct(grid_adjoint.shape, f32),
            jax.ShapeDtypeStruct(spectral.shape, f32),
        ),
        in_specs=[hbm, hbm, hbm, vmem],
        out_specs=(hbm, hbm),
        scratch_shapes=[
            pltpu.VMEM((devices, 2 * levels, lats), f32),
            pltpu.VMEM((lats * levels, LANES), f32),
            pltpu.VMEM((lats * levels, 2 * LANES), bf16),
            pltpu.VMEM((2 * LANES, longitudes), bf16),
            pltpu.VMEM((2, wide, lats // PIECES * levels, LANES), f32),
            pltpu.VMEM((2, lats // PIECES, levels, longitudes), f32),
            pltpu.VMEM(spectral.shape, f32),
            dma, dma((2,)), dma((2,)), dma, dma,
        ],
        compiler_params=pltpu.CompilerParams(vmem_limit_bytes=67_043_328),
        name="finish",
    )(returned, partial, spectral, waves)
    return spectral.reshape(slots, 2, every, depth).transpose(0, 3, 1, 2), grid


def solution(mesh):
    return jax.shard_map(
        shards,
        mesh=mesh,
        in_specs=(
            P("band", "lev", None),
            P("band", "lev", None),
            P(("band", "lev"), None, None),
            P(),
            P(("band", "lev"), None, None, None),
            P(),
            P(),
            P(),
        ),
        out_specs=(P(("band", "lev"), None, None, None), P("band", "lev", None)),
        check_vma=False,
    )
```

time: 476 us -> 440 us (0.924)
  Pallas kernels: 456 us -> 435 us
  local copies, waits for them, and re-layouts: 12.9 us -> 3.76 us
  other arithmetic: 6.35 us -> 0 us
    pallas_call x1, Pallas kernels: 68.9 us -> 22.9 us  [shards(): pl.pallas_call(functools.partial(finish_kernel, dims), out_shape=(jax.Sha...]
    pallas_call x1, Pallas kernels: 387 us -> 412 us  [shards(): pl.pallas_call(functools.partial(forward_kernel, dims), out_shape=(jax.Sh...]
    unnamed x1 -> x0, local copies, waits for them, and re-layouts: 4.91 us -> none
where the time goes in v2:
time: 440 us; the launch traced here: 439 us
  Pallas kernels  435 us (99%)
    pallas_call x1, Pallas kernels, shards(): pl.pallas_call(functools.partial(forward_kernel, dims), out_shape=(jax.Sh...  412 us
    pallas_call x1, Pallas kernels, shards(): pl.pallas_call(functools.partial(finish_kernel, dims), out_shape=(jax.Sha...  22.9 us

profile of v2, /device:TPU:0, one launch (start us, length us, event | category | flops | bytes accessed | tf_op | source)
XLA Modules:
  0.0 439.4 jit_solution(10690578627551962458)
XLA Ops:
  0.6 0.7 broadcast_in_dim.23
  1.3 0.1 broadcast_in_dim.24
  1.4 0.7 broadcast_in_dim.25.rate_ref
  2.1 0.8 reshape.19
  2.9 0.2 broadcast_in_dim.20
  3.1 0.2 broadcast_in_dim.21
  3.4 1.0 broadcast_in_dim.22.wave_ref
  4.4 412.0 %spectral.1 = (f32[16,128,512]{2,1,0:T(8,128)}, f32[32,512,128]{2,1,0:T(8,128)}, f32[16,2048,128]{2,1,0:T(8,128)}) custom-call(f32[128,16,2048]{2,1,0:T(8,128)} %grid_ref.1, f32[128,16,2048]{2,1,0:T(8,128)} %traj_ref.1, s32[1024,128]{1,0:T(8,128)} %broadcast_in_dim.22.wave_ref, f32[16,512,512]{2,1,0:T(8,128)} %leg_ref.1, f32[16,128,512]{2,1,0:T(8,128)} %bitcast.7, ...), custom_call_target="tpu_custom_call" | custom-call | tf_op jit(solution)/shard_map/spectral/pallas_call | solution.py:652
  416.4 22.9 %finish.1 = (f32[128,16,2048]{2,1,0:T(8,128)}, f32[16,128,512]{2,1,0:T(8,128)}) custom-call(f32[32,512,128]{2,1,0:T(8,128)} %get-tuple-element.7.returned, f32[16,2048,128]{2,1,0:T(8,128)} %get-tuple-element.8.partial, f32[16,128,512]{2,1,0:T(8,128)} %get-tuple-element.9.spectral, s32[1024,128]{1,0:T(8,128)} %broadcast_in_dim.22.wave_ref), custom_call_target="tpu_custom_call" | custom-call | tf_op jit(solution)/shard_map/finish/pallas_call | solution.py:688
  (1 shorter events, 0.0 us)

commit v3 on v2

--- a/solution.py
+++ b/solution.py
@@ -114,6 +114,7 @@
 PAIR = 2
 PIECES = 8
 GROUP = 4
+KEEP = 48_000_000
 NN = (((1,), (0,)), ((), ()))
 NT = (((1,), (1,)), ((), ()))
 
@@ -175,11 +176,11 @@
 def forward_kernel(
     dims,
     grid_ref, traj_ref, wave_ref, leg_ref, state_ref, rate_ref, to_ref, from_ref,
-    spec_out, returned, partial,
-    high, low, forced, stage, traj, rows_h, rows_l, sending, arrived, synth, leg, state, spec,
-    into, outof, back, pulled, turned,
+    spec_out, returned, forced,
+    high, low, stage, traj, rows_h, rows_l, sending, arrived, synth, leg, state, spec,
+    into, outof, back, flat_h, flat_l,
     grid_sem, traj_sem, send_sem, recv_sem, send2_sem, recv2_sem, leg_sem, state_sem, spec_sem,
-    pull_sem, part_sem,
+    pull_sem,
 ):
     bands, parts, lats, levels, longitudes, slots, depth, half = dims
     devices = bands * parts
@@ -190,6 +191,7 @@
     small = 2 * GROUP
     tall = devices * small
     groups = slots // GROUP
+    count_rows = devices * unit
     wide = longitudes // LANES
     band, lev = lax.axis_index("band"), lax.axis_index("lev")
     me = band * parts + lev
@@ -442,50 +444,54 @@
 
     lax.fori_loop(0, slots, one_slot, 0)
 
-    block = 256
-
-    def part_copy(m):
-        at = aligned(m * block, block)
-        return pltpu.make_async_copy(forced.at[:, at, :], partial.at[:, at, :], part_sem)
+    staged = devices * GROUP * each
+    pulled = arrived.reshape(levels * count_rows // (GROUP * each), GROUP * each, lats)
+    block = 1024
 
     for g in range(groups):
         last = g == groups - 1
         rows = (GROUP - 1 if last else GROUP) * each
         here = returned.at[:, g * GROUP * each : g * GROUP * each + rows, :]
-        into_vmem = pulled.at[:, 0:rows, :]
         pltpu.make_async_copy(here, here, recv2_sem.at[g]).wait()
-        copy = pltpu.make_async_copy(here, into_vmem, pull_sem)
+        copy = pltpu.make_async_copy(here, pulled.at[0:devices, 0:rows, :], pull_sem)
         copy.start()
         copy.wait()
-        flat = pulled.reshape(devices * GROUP * each, lats)
 
         def pull(l, carry):
-            x = flat[pl.ds(l, tall, stride=levels), :]
+            x = arrived[pl.ds(l, tall, stride=levels), :]
             if last:
                 row = lax.rem(lax.broadcasted_iota(jnp.int32, x.shape, 0), small)
                 x = jnp.where(row < small - 2, x, 0.0)
             x = x.T
             for j in range(tall // LANES):
-                turned[j, pl.ds(l, lats, stride=levels), :] = x[:, j * LANES : (j + 1) * LANES]
+                arrived[pl.ds(staged + j * lats * levels + l, lats, stride=levels), :] = x[
+                    :, j * LANES : (j + 1) * LANES
+                ]
             return carry
 
         lax.fori_loop(0, levels, pull, 0)
 
+        def split(r, carry):
+            lat = jnp.where(south, lats - 1 - r, r)
+            to = aligned(r * levels, levels)
+            for j in range(tall // LANES):
+                x = arrived[aligned(staged + (j * lats + lat) * levels, levels), :]
+                h, l = halves_of(x)
+                flat_h[to, j * LANES : (j + 1) * LANES] = h
+                flat_l[to, j * LANES : (j + 1) * LANES] = l
+            return carry
+
+        lax.fori_loop(0, lats, split, 0)
+
         def multiply(m, carry):
-            for r in range(block // levels):
-                to = m * (block // levels) + r
-                lat = jnp.where(south, lats - 1 - to, to)
-                for j in range(tall // LANES):
-                    h, l = halves_of(turned[j, aligned(lat * levels, levels), :])
-                    rows_h[r * levels : (r + 1) * levels, j * LANES : (j + 1) * LANES] = h
-                    rows_l[r * levels : (r + 1) * levels, j * LANES : (j + 1) * LANES] = l
-            ah, al = rows_h[:block, :tall], rows_l[:block, :tall]
             at = aligned(m * block, block)
 
             def inner(w, c):
                 cut = aligned(w * 2 * LANES, 2 * LANES)
                 rows_at = slice(g * tall, (g + 1) * tall)
-                got = dot3((ah, al), (high[rows_at, cut], low[rows_at, cut]), NN)
+                got = dot3(
+                    (flat_h[at, :], flat_l[at, :]), (high[rows_at, cut], low[rows_at, cut]), NN
+                )
                 for j in range(2):
                     x = got[:, j * LANES : (j + 1) * LANES]
                     if g > 0:
@@ -494,15 +500,12 @@
                 return c
 
             lax.fori_loop(0, wide // 2, inner, 0)
-            if last:
-                part_copy(m).start()
             return carry
 
         lax.fori_loop(0, lats * levels // block, multiply, 0)
 
     for s in range(max(slots - 2, 0), slots):
         pltpu.make_async_copy(spec.at[s % 2], spec_out.at[s], spec_sem.at[s % 2]).wait()
-    pltpu.make_async_copy(forced, partial, part_sem).wait()
     sent = pl.ds(0, pairs * (devices - 1) * message)
     pltpu.make_async_copy(sending.at[sent, :], sending.at[sent, :], send_sem).wait()
     sent = pl.ds(0, slots * (devices - 1) * each)
@@ -513,8 +516,8 @@
 
 def finish_kernel(
     dims, returned, partial, spectral, wave_ref, grid_out, spec_out,
-    pulled, turned, stacked, table, before, result, spec,
-    pull_sem, in_sem, out_sem, spec_in, spec_done,
+    pulled, turned, stacked, table, result, spec,
+    pull_sem, out_sem, spec_in, spec_done,
 ):
     bands, parts, lats, levels, longitudes, slots, depth, half = dims
     devices = bands * parts
@@ -525,10 +528,6 @@
     span = lats // PIECES
     block = span * levels
 
-    def in_copy(m, slot):
-        at = aligned(m * block, block)
-        return pltpu.make_async_copy(partial.at[:, at, :], before.at[slot], in_sem.at[slot])
-
     def out_copy(m, slot):
         return pltpu.make_async_copy(
             result.at[slot], grid_out.at[aligned(m * span, span), :, :], out_sem.at[slot]
@@ -538,8 +537,6 @@
         returned.at[:, (slots - 1) * each : slots * each, :], pulled, pull_sem
     )
     pull.start()
-    in_copy(0, 0).start()
-    in_copy(1, 1).start()
     spec_copy = pltpu.make_async_copy(spectral, spec, spec_in)
     spec_copy.start()
 
@@ -579,29 +576,24 @@
 
     def outer(m, carry):
         slot = lax.rem(m, 2)
-        in_copy(m, slot).wait()
-
         @pl.when(m >= 2)
         def _():
             out_copy(m - 2, slot).wait()
 
-        a = stacked[aligned(m * block, block), :]
+        at = aligned(m * block, block)
+        a = stacked[at, :]
 
         def inner(w, c):
             cut = aligned(w * 2 * LANES, 2 * LANES)
             got = dot1(a, table[:, cut], NN)
             for j in range(2):
-                x = got[:, j * LANES : (j + 1) * LANES] + before[slot, 2 * w + j]
+                x = got[:, j * LANES : (j + 1) * LANES] + partial[2 * w + j, at, :]
                 to = aligned((2 * w + j) * LANES, LANES)
                 result[slot, :, :, to] = x.reshape(span, levels, LANES)
             return c
 
         lax.fori_loop(0, wide // 2, inner, 0)
         out_copy(m, slot).start()
-
-        @pl.when(m + 2 < PIECES)
-        def _():
-            in_copy(m + 2, slot).start()
 
         return carry
 
@@ -654,14 +646,13 @@
         out_shape=(
             jax.ShapeDtypeStruct((slots, 2 * every, depth), f32),
             jax.ShapeDtypeStruct((devices, slots * 2 * levels, lats), f32),
-            jax.ShapeDtypeStruct((wide, lats * levels, LANES), f32),
+            pltpu.VMEM((wide, lats * levels, LANES), f32),
         ),
         in_specs=[hbm, hbm, vmem, hbm, hbm, vmem, vmem, vmem],
-        out_specs=(hbm, hbm, hbm),
+        out_specs=(hbm, hbm, vmem),
         scratch_shapes=[
             pltpu.VMEM((count, longitudes), bf16),
             pltpu.VMEM((count, longitudes), bf16),
-            pltpu.VMEM((wide, levels * lats, LANES), f32),
             pltpu.VMEM((2, lats // PIECES, SUB, longitudes), f32),
             pltpu.VMEM((2, lats // PIECES, SUB, longitudes), f32),
             pltpu.VMEM((PAIR * lats, longitudes), bf16),
@@ -673,13 +664,13 @@
             pltpu.VMEM((2, 2 * every, depth), f32),
             pltpu.VMEM((2, 2 * every, depth), f32),
             square, square, square,
-            pltpu.VMEM((devices, GROUP * 2 * levels, lats), f32),
-            pltpu.VMEM((devices * 2 * GROUP // LANES, lats * levels, LANES), f32),
+            pltpu.VMEM((lats * levels, devices * 2 * GROUP), bf16),
+            pltpu.VMEM((lats * levels, devices * 2 * GROUP), bf16),
             dma((2,)), dma((2,)), dma, dma, dma, dma((slots // GROUP + 1,)),
-            dma((2,)), dma((2,)), dma((2,)), dma, dma,
+            dma((2,)), dma((2,)), dma((2,)), dma,
         ],
         compiler_params=pltpu.CompilerParams(
-            collective_id=0, has_side_effects=True, vmem_limit_bytes=67_043_328
+            collective_id=0, has_side_effects=True, vmem_limit_bytes=KEEP
         ),
         name="spectral",
     )(
@@ -691,19 +682,18 @@
             jax.ShapeDtypeStruct(grid_adjoint.shape, f32),
             jax.ShapeDtypeStruct(spectral.shape, f32),
         ),
-        in_specs=[hbm, hbm, hbm, vmem],
+        in_specs=[hbm, vmem, hbm, vmem],
         out_specs=(hbm, hbm),
         scratch_shapes=[
             pltpu.VMEM((devices, 2 * levels, lats), f32),
             pltpu.VMEM((lats * levels, LANES), f32),
             pltpu.VMEM((lats * levels, 2 * LANES), bf16),
             pltpu.VMEM((2 * LANES, longitudes), bf16),
-            pltpu.VMEM((2, wide, lats // PIECES * levels, LANES), f32),
             pltpu.VMEM((2, lats // PIECES, levels, longitudes), f32),
             pltpu.VMEM(spectral.shape, f32),
-            dma, dma((2,)), dma((2,)), dma, dma,
+            dma, dma((2,)), dma, dma,
         ],
-        compiler_params=pltpu.CompilerParams(vmem_limit_bytes=67_043_328),
+        compiler_params=pltpu.CompilerParams(vmem_limit_bytes=KEEP),
         name="finish",
     )(returned, partial, spectral, waves)
     return spectral.reshape(slots, 2, every, depth).transpose(0, 3, 1, 2), grid

time: 440 us -> 435 us (0.989)
  Pallas kernels: 435 us -> 422 us
  local copies, waits for them, and re-layouts: 3.76 us -> 11.6 us
    pallas_call x1, Pallas kernels: 412 us -> 397 us  [shards(): pl.pallas_call(functools.partial(forward_kernel, dims), out_shape=(jax.Sh...]
    unnamed x0 -> x6, local copies, waits for them, and re-layouts: none -> 7.91 us
where the time goes in v3:
time: 435 us; the launch traced here: 434 us
  Pallas kernels  422 us (97%)
  local copies, waits for them, and re-layouts  11.6 us (3%)
    pallas_call x1, Pallas kernels, shards(): pl.pallas_call(functools.partial(forward_kernel, dims), out_shape=(jax.Sh...  397 us
    pallas_call x1, Pallas kernels, shards(): pl.pallas_call(functools.partial(finish_kernel, dims), out_shape=(jax.Sha...  24.6 us

profile of v3, /device:TPU:0, one launch (start us, length us, event | category | flops | bytes accessed | tf_op | source)
XLA Modules:
  0.0 434.1 jit_solution(14344645512336943550)
XLA Ops:
  0.6 0.7 broadcast_in_dim.23
  1.3 0.1 broadcast_in_dim.24
  1.4 0.7 broadcast_in_dim.25.rate_ref
  2.1 0.8 reshape.19
  2.9 0.2 broadcast_in_dim.20
  3.1 0.2 broadcast_in_dim.21
  3.4 1.0 broadcast_in_dim.22.wave_ref
  4.4 0.0 copy-start.1
  4.4 397.2 %spectral.1 = (f32[16,128,512]{2,1,0:T(8,128)}, f32[32,512,128]{2,1,0:T(8,128)}, f32[16,2048,128]{2,1,0:T(8,128)S(1)}) custom-call(f32[128,16,2048]{2,1,0:T(8,128)} %grid_ref.1, f32[128,16,2048]{2,1,0:T(8,128)} %traj_ref.1, s32[1024,128]{1,0:T(8,128)} %broadcast_in_dim.22.wave_ref, f32[16,512,512]{2,1,0:T(8,128)} %leg_ref.1, f32[16,128,512]{2,1,0:T(8,128)} %bitcast.7, ...), custom_call_target="tpu_custom_call" | custom-call | tf_op jit(solution)/shard_map/spectral/pallas_call | solution.py:644
  401.6 0.0 copy-start
  401.6 5.7 %copy-done = f32[16,2048,128]{2,1,0:T(8,128)} copy-done((f32[16,2048,128]{2,1,0:T(8,128)}, f32[16,2048,128]{2,1,0:T(8,128)S(1)}, u32[]{:S(2)}) %copy-start) | copy-done | bytes 16777240
  407.3 0.0 copy-done.1
  407.3 0.0 copy-start.2
  407.3 2.2 copy-done.2
  409.5 24.6 %finish.1 = (f32[128,16,2048]{2,1,0:T(8,128)}, f32[16,128,512]{2,1,0:T(8,128)}) custom-call(f32[32,512,128]{2,1,0:T(8,128)} %get-tuple-element.7.returned, f32[16,2048,128]{2,1,0:T(8,128)} %copy-done, f32[16,128,512]{2,1,0:T(8,128)S(1)} %copy-done.2, s32[1024,128]{1,0:T(8,128)S(1)} %copy-done.1), custom_call_target="tpu_custom_call" | custom-call | tf_op jit(solution)/shard_map/finish/pallas_call | solution.py:679
  (1 shorter events, 0.0 us)
Async XLA Ops:
  4.4 403.0 %copy-start.1 = (s32[1024,128]{1,0:T(8,128)S(1)}, s32[1024,128]{1,0:T(8,128)}, u32[]{:S(2)}) copy-start(s32[1024,128]{1,0:T(8,128)} %broadcast_in_dim.22.wave_ref) | copy-start | bytes 1572868
  401.6 5.7 %copy-start = (f32[16,2048,128]{2,1,0:T(8,128)}, f32[16,2048,128]{2,1,0:T(8,128)S(1)}, u32[]{:S(2)}) copy-start(f32[16,2048,128]{2,1,0:T(8,128)S(1)} %get-tuple-element.8.partial) | copy-start | bytes 50331652
  407.3 2.2 copy-start.2

commit v4 on v3

--- a/solution.py
+++ b/solution.py
@@ -114,7 +114,9 @@
 PAIR = 2
 PIECES = 8
 GROUP = 4
-KEEP = 48_000_000
+BLOCKS = 4
+GRANT = 50_000_000
+LAST_GRANT = 44_000_000
 NN = (((1,), (0,)), ((), ()))
 NT = (((1,), (1,)), ((), ()))
 
@@ -139,8 +141,8 @@
 
 def circle(phase, longitudes):
     quarter = longitudes // 4
-    quadrant = phase // quarter
-    rest = phase - quadrant * quarter
+    quadrant = phase >> (quarter.bit_length() - 1)
+    rest = phase & (quarter - 1)
     flip = rest > quarter // 2
     angle = jnp.where(flip, quarter - rest, rest).astype(jnp.float32) * (
         2.0 * math.pi / longitudes
@@ -153,7 +155,7 @@
         -0.5 + z * (1 / 24 + z * (-1 / 720 + z * (1 / 40320 + z * (-1 / 3628800))))
     )
     c, s = jnp.where(flip, sine, cosine), jnp.where(flip, cosine, sine)
-    odd = lax.rem(quadrant, 2) == 1
+    odd = (quadrant & 1) == 1
     c, s = jnp.where(odd, s, c), jnp.where(odd, c, s)
     c = jnp.where((quadrant == 1) | (quadrant == 2), -c, c)
     return c, jnp.where(quadrant >= 2, -s, s)
@@ -161,8 +163,8 @@
 
 def table_rows(waves, imaginary, longitudes):
     column = lax.broadcasted_iota(jnp.int32, waves.shape, 1)
-    ca, sa = circle(lax.rem(waves * (column * LANES), longitudes), longitudes)
-    cb, sb = circle(lax.rem(waves * column, longitudes), longitudes)
+    ca, sa = circle((waves * (column * LANES)) & (longitudes - 1), longitudes)
+    cb, sb = circle((waves * column) & (longitudes - 1), longitudes)
     scale = float(longitudes) ** -0.5
     ca, sa = ca * scale, sa * scale
     p = jnp.where(imaginary, -sa, ca)
@@ -173,12 +175,56 @@
     ]
 
 
+def wave_columns(slot_ref, own):
+    for i in range(slot_ref.shape[0]):
+        row = jnp.broadcast_to(slot_ref[i : i + 1, :].astype(jnp.float32), (LANES, LANES))
+        own[i * LANES : (i + 1) * LANES, :] = row.T.astype(jnp.int32)
+
+
+def single_table(waves, table, longitudes):
+    devices = waves.shape[0]
+    waves = jnp.concatenate([waves, waves], axis=0)
+    imaginary = lax.broadcasted_iota(jnp.int32, waves.shape, 0) >= devices
+    short = 2 * devices
+    for i, (h, l) in enumerate(table_rows(waves, imaginary, longitudes)):
+        cut = slice(i * LANES, (i + 1) * LANES)
+        table[0:short, cut] = h
+        table[short : 2 * short, cut] = l
+        table[2 * short : 3 * short, cut] = h
+        table[3 * short : 4 * short, cut] = jnp.zeros_like(h)
+
+
+def single_rows(dims, south, flat, turned, base, stacked):
+    bands, parts, lats, levels = dims[:4]
+    devices = bands * parts
+
+    def gather(l, carry):
+        x = jnp.concatenate(
+            [flat[pl.ds(c * levels + l, devices, stride=2 * levels), :] for c in range(2)], axis=0
+        )
+        turned[pl.ds(base + l, lats, stride=levels), :] = jnp.concatenate([x, x], axis=0).T
+        return carry
+
+    lax.fori_loop(0, levels, gather, 0)
+    keep = lax.broadcasted_iota(jnp.int32, (levels, LANES), 1) < 2 * devices
+
+    def split(r, carry):
+        lat = jnp.where(south, lats - 1 - r, r)
+        h, l = halves_of(turned[aligned(base + lat * levels, levels), :])
+        to = aligned(r * levels, levels)
+        stacked[to, 0:LANES] = h
+        stacked[to, LANES : 2 * LANES] = jnp.where(keep, l, jnp.zeros_like(l))
+        return carry
+
+    lax.fori_loop(0, lats, split, 0)
+
+
 def forward_kernel(
     dims,
-    grid_ref, traj_ref, wave_ref, leg_ref, state_ref, rate_ref, to_ref, from_ref,
+    grid_ref, traj_ref, slot_ref, leg_ref, state_ref, rate_ref, to_ref, from_ref,
     spec_out, returned, forced,
     high, low, stage, traj, rows_h, rows_l, sending, arrived, synth, leg, state, spec,
-    into, outof, back, flat_h, flat_l,
+    into, outof, back, flat_h, flat_l, wave_own, wave_ref, rate_col, single,
     grid_sem, traj_sem, send_sem, recv_sem, send2_sem, recv2_sem, leg_sem, state_sem, spec_sem,
     pull_sem,
 ):
@@ -258,18 +304,140 @@
     def state_copy(s, slot):
         return pltpu.make_async_copy(state_ref.at[s], state.at[slot], state_sem.at[slot])
 
+    wave_columns(slot_ref, wave_own)
+    for g in range(groups):
+        for i in range(GROUP):
+            x = wave_own[pl.ds(g * GROUP + i, devices, stride=slots), :]
+            for c in range(2):
+                wave_ref[pl.ds(g * tall + 2 * i + c, devices, stride=small), :] = x
+    rate = jnp.concatenate([rate_ref[...], rate_ref[...]], axis=1)
+    rate_col[...] = jnp.broadcast_to(rate, (2 * every, 2 * every)).T
     block_rows = 64
 
     def fill(r, carry):
         at = aligned(r * block_rows, block_rows)
         waves = wave_ref[at, :]
-        imaginary = lax.rem(lax.broadcasted_iota(jnp.int32, waves.shape, 0), 2) == 1
+        imaginary = (lax.broadcasted_iota(jnp.int32, waves.shape, 0) & 1) == 1
         for i, (h, l) in enumerate(table_rows(waves, imaginary, longitudes)):
             high[at, i * LANES : (i + 1) * LANES] = h
             low[at, i * LANES : (i + 1) * LANES] = l
         return carry
 
-    lax.fori_loop(0, devices * unit // block_rows, fill, 0)
+    def greeted_copy(source, target, d, sem):
+        return pltpu.make_async_remote_copy(
+            src_ref=sending.at[source, :],
+            dst_ref=arrived.at[target, :],
+            send_sem=send_sem,
+            recv_sem=recv_sem.at[sem],
+            device_id=mesh_id(d),
+            device_id_type=pl.DeviceIdType.MESH,
+        )
+
+    def partner(i):
+        return jnp.bitwise_xor(me, devices - 1 - i)
+
+    def send_pair(q):
+        to = aligned((me * pairs + q) * message, message)
+
+        def body(i, carry):
+            d = partner(i)
+            greeted_copy(aligned((q * devices + d) * message, message), to, d, 0).start()
+            return carry
+
+        lax.fori_loop(0, devices - 1, body, 0)
+        pltpu.make_async_copy(
+            sending.at[aligned((q * devices + me) * message, message), :],
+            arrived.at[to, :],
+            recv_sem.at[0],
+        ).start()
+
+    def send_part(q, r, sem):
+        def cut(first, h):
+            return aligned(first * message + h * unit + r * small, small)
+
+        def body(i, carry):
+            d = partner(i)
+            for h in range(PAIR):
+                greeted_copy(
+                    cut(q * devices + d, h), cut(me * pairs + q, h), d, sem
+                ).start()
+            return carry
+
+        lax.fori_loop(0, devices - 1, body, 0)
+        for h in range(PAIR):
+            pltpu.make_async_copy(
+                sending.at[cut(q * devices + me, h), :],
+                arrived.at[cut(me * pairs + q, h), :],
+                recv_sem.at[sem],
+            ).start()
+
+    def extract(q):
+        first = q * PAIR
+        block, local = first // SUB, lax.rem(first, SUB)
+        for h in range(PAIR):
+            for i in range(wide):
+                x = forced[i, pl.ds(block * lats * SUB + local + h, lats, stride=SUB), :]
+                rh, rl = halves_of(x)
+                rows_h[h * lats : (h + 1) * lats, i * LANES : (i + 1) * LANES] = rh
+                rows_l[h * lats : (h + 1) * lats, i * LANES : (i + 1) * LANES] = rl
+
+    def transform(q, r):
+        at = aligned(r * tall, tall)
+        got = dot3((high[at, :], low[at, :]), (rows_h[...], rows_l[...]), NT)
+        for d in range(devices):
+            for h in range(PAIR):
+                to = (q * devices + d) * message + h * unit + r * small
+                sending[aligned(to, small), :] = got[
+                    d * small : (d + 1) * small, h * lats : (h + 1) * lats
+                ]
+
+    per = SUB // PAIR
+    blocks = levels // SUB
+
+    def finish(i, c):
+        finish_piece(i)
+        return c
+
+    lax.fori_loop(0, PIECES, finish, 0)
+    extract(jnp.int32(0))
+
+    def opening(r, carry):
+        lax.fori_loop(r * (tall // block_rows), (r + 1) * (tall // block_rows), fill, 0)
+        transform(0, r)
+
+        @pl.when(r == 0)
+        def _():
+            pl.semaphore_wait(barrier, devices - 1)
+
+        send_part(0, r, 0)
+        return carry
+
+    lax.fori_loop(0, groups, opening, 0)
+
+    def middle(q, carry):
+        @pl.when(lax.rem(q, per) == 0)
+        def _():
+            lax.fori_loop(q // per * PIECES, (q // per + 1) * PIECES, finish, 0)
+
+        extract(q)
+
+        def each_group(r, c):
+            transform(q, r)
+            return c
+
+        lax.fori_loop(0, groups, each_group, 0)
+        send_pair(q)
+        return carry
+
+    lax.fori_loop(1, pairs - 1, middle, 0)
+    extract(jnp.int32(pairs - 1))
+
+    def closing(r, carry):
+        transform(pairs - 1, r)
+        send_part(pairs - 1, r, r + 1)
+        return carry
+
+    lax.fori_loop(0, groups, closing, 0)
     for m in (into, outof, back):
         m[...] = jnp.zeros_like(m)
     for c in range(2):
@@ -280,84 +448,17 @@
             at = (2 * p + c) * levels
             back[at : at + levels, cut] = from_ref[p * levels : (p + 1) * levels, :]
 
-    def send_copy(q, d):
-        return pltpu.make_async_remote_copy(
-            src_ref=sending.at[aligned((q * devices + d) * message, message), :],
-            dst_ref=arrived.at[aligned((me * pairs + q) * message, message), :],
-            send_sem=send_sem,
-            recv_sem=recv_sem,
-            device_id=mesh_id(d),
-            device_id_type=pl.DeviceIdType.MESH,
-        )
-
-    def transform(q):
-        first = q * PAIR
-        block, local = first // SUB, lax.rem(first, SUB)
-        for h in range(PAIR):
-            for i in range(wide):
-                x = forced[i, pl.ds(block * lats * SUB + local + h, lats, stride=SUB), :]
-                rh, rl = halves_of(x)
-                rows_h[h * lats : (h + 1) * lats, i * LANES : (i + 1) * LANES] = rh
-                rows_l[h * lats : (h + 1) * lats, i * LANES : (i + 1) * LANES] = rl
-
-        def body(r, carry):
-            at = aligned(r * tall, tall)
-            got = dot3((high[at, :], low[at, :]), (rows_h[...], rows_l[...]), NT)
-            for d in range(devices):
-                for h in range(PAIR):
-                    to = (q * devices + d) * message + h * unit + r * small
-                    sending[aligned(to, small), :] = got[
-                        d * small : (d + 1) * small, h * lats : (h + 1) * lats
-                    ]
-            return carry
-
-        lax.fori_loop(0, groups, body, 0)
-
-    def send_pair(q):
-        def body(i, carry):
-            send_copy(q, jnp.bitwise_xor(me, devices - 1 - i)).start()
-            return carry
-
-        lax.fori_loop(0, devices - 1, body, 0)
-        pltpu.make_async_copy(
-            sending.at[aligned((q * devices + me) * message, message), :],
-            arrived.at[aligned((me * pairs + q) * message, message), :],
-            recv_sem,
-        ).start()
-
-    per = SUB // PAIR
-
-    def outer(block, carry):
-        def finish(i, c):
-            finish_piece(block * PIECES + i)
-            return c
-
-        lax.fori_loop(0, PIECES, finish, 0)
-
-        def run(j, c):
-            q = block * per + j
-            transform(q)
-
-            @pl.when(q == 0)
-            def _():
-                pl.semaphore_wait(barrier, devices - 1)
-
-            send_pair(q)
-            return c
-
-        lax.fori_loop(0, per, run, 0)
-        return carry
-
-    lax.fori_loop(0, levels // SUB, outer, 0)
-
     leg_copy(0, 0).start()
     state_copy(0, 0).start()
-    pltpu.make_async_copy(arrived, arrived, recv_sem).wait()
+    before = arrived.at[pl.ds(0, (pairs - 1) * devices * message), :]
+    pltpu.make_async_copy(before, before, recv_sem.at[0]).wait()
+    last_part = arrived.at[pl.ds(0, devices * PAIR * small), :]
 
     lane = lax.broadcasted_iota(jnp.int32, (2 * every, depth), 1)
     even = lax.rem(lane, 2) == 0
     folds = bands // 2
     each = 2 * levels
+    whole = slots - GROUP
 
     def column(b, s):
         return jnp.concatenate(
@@ -380,7 +481,11 @@
 
     def one_slot(s, carry):
         slot = lax.rem(s, 2)
-        sem = jnp.where(s == slots - 1, groups, s // GROUP)
+        sem = jnp.where(s < whole, s // GROUP, groups - 1 + s - whole)
+
+        @pl.when(lax.rem(s, GROUP) == 0)
+        def _():
+            pltpu.make_async_copy(last_part, last_part, recv_sem.at[s // GROUP + 1]).wait()
 
         @pl.when(s + 1 < slots)
         def _():
@@ -409,7 +514,7 @@
         helm = degree * (degree + 1.0) / (depth * (depth - 1.0))
         total = jnp.where(order < depth - wave, analysed + state[slot], 0.0)
         modes = dot3(halves_of(into[...]), halves_of(total), NN)
-        scaled = halves_of(modes / (1.0 + helm * rate_ref[:, 0:1]))
+        scaled = halves_of(modes / (1.0 + helm * rate_col[:, 0:1]))
 
         @pl.when(s >= 2)
         def _():
@@ -431,7 +536,7 @@
             synth[aligned(base + (bands - 1 - b) * 2 * every, 2 * every), :] = other[:, cut]
 
         def body(i, c):
-            send2_copy(s, jnp.bitwise_xor(me, devices - 1 - i), sem).start()
+            send2_copy(s, partner(i), sem).start()
             return c
 
         lax.fori_loop(0, devices - 1, body, 0)
@@ -448,10 +553,9 @@
     pulled = arrived.reshape(levels * count_rows // (GROUP * each), GROUP * each, lats)
     block = 1024
 
-    for g in range(groups):
-        last = g == groups - 1
-        rows = (GROUP - 1 if last else GROUP) * each
-        here = returned.at[:, g * GROUP * each : g * GROUP * each + rows, :]
+    for g in range(groups - 1):
+        rows = GROUP * each
+        here = returned.at[:, g * rows : (g + 1) * rows, :]
         pltpu.make_async_copy(here, here, recv2_sem.at[g]).wait()
         copy = pltpu.make_async_copy(here, pulled.at[0:devices, 0:rows, :], pull_sem)
         copy.start()
@@ -459,9 +563,6 @@
 
         def pull(l, carry):
             x = arrived[pl.ds(l, tall, stride=levels), :]
-            if last:
-                row = lax.rem(lax.broadcasted_iota(jnp.int32, x.shape, 0), small)
-                x = jnp.where(row < small - 2, x, 0.0)
             x = x.T
             for j in range(tall // LANES):
                 arrived[pl.ds(staged + j * lats * levels + l, lats, stride=levels), :] = x[
@@ -504,6 +605,37 @@
 
         lax.fori_loop(0, lats * levels // block, multiply, 0)
 
+    thin = arrived.reshape(levels * count_rows // each, each, lats)
+
+    def lone(i, carry):
+        s = whole + i
+        single_table(wave_own[pl.ds(s, devices, stride=slots), :], single, longitudes)
+        here = returned.at[:, aligned(s * each, each), :]
+        pltpu.make_async_copy(here, here, recv2_sem.at[groups - 1 + i]).wait()
+        copy = pltpu.make_async_copy(here, thin.at[0:devices], pull_sem)
+        copy.start()
+        copy.wait()
+        single_rows(dims, south, arrived, arrived, staged, flat_h)
+
+        def multiply(m, carry):
+            at = aligned(m * block, block)
+
+            def inner(w, c):
+                got = dot1(flat_h[at, :], single[:, aligned(w * 2 * LANES, 2 * LANES)], NN)
+                for j in range(2):
+                    forced[2 * w + j, at, :] = (
+                        forced[2 * w + j, at, :] + got[:, j * LANES : (j + 1) * LANES]
+                    )
+                return c
+
+            lax.fori_loop(0, wide // 2, inner, 0)
+            return carry
+
+        lax.fori_loop(0, lats * levels // block, multiply, 0)
+        return carry
+
+    lax.fori_loop(0, GROUP - 1, lone, 0)
+
     for s in range(max(slots - 2, 0), slots):
         pltpu.make_async_copy(spec.at[s % 2], spec_out.at[s], spec_sem.at[s % 2]).wait()
     sent = pl.ds(0, pairs * (devices - 1) * message)
@@ -511,21 +643,20 @@
     sent = pl.ds(0, slots * (devices - 1) * each)
     pltpu.make_async_copy(synth.at[sent, :], synth.at[sent, :], send2_sem).wait()
     final = returned.at[:, (slots - 1) * each : slots * each, :]
-    pltpu.make_async_copy(final, final, recv2_sem.at[groups]).wait()
+    pltpu.make_async_copy(final, final, recv2_sem.at[groups - 1 + GROUP - 1]).wait()
 
 
 def finish_kernel(
-    dims, returned, partial, spectral, wave_ref, grid_out, spec_out,
-    pulled, turned, stacked, table, result, spec,
+    dims, returned, partial, spectral, slot_ref, grid_out, spec_out,
+    pulled, turned, stacked, table, result, spec, wave_own,
     pull_sem, out_sem, spec_in, spec_done,
 ):
     bands, parts, lats, levels, longitudes, slots, depth, half = dims
     devices = bands * parts
     each = 2 * levels
-    small = 2 * GROUP
     wide = longitudes // LANES
     south = lax.axis_index("band") >= bands // 2
-    span = lats // PIECES
+    span = lats // BLOCKS
     block = span * levels
 
     def out_copy(m, slot):
@@ -540,39 +671,10 @@
     spec_copy = pltpu.make_async_copy(spectral, spec, spec_in)
     spec_copy.start()
 
-    first = (slots // GROUP - 1) * devices * small + small - 2
-    waves = wave_ref[pl.ds(first, devices, stride=small), :]
-    waves = jnp.concatenate([waves, waves], axis=0)
-    imaginary = lax.broadcasted_iota(jnp.int32, waves.shape, 0) >= devices
-    short = 2 * devices
-    for i, (h, l) in enumerate(table_rows(waves, imaginary, longitudes)):
-        cut = slice(i * LANES, (i + 1) * LANES)
-        table[0:short, cut] = h
-        table[short : 2 * short, cut] = l
-        table[2 * short : 3 * short, cut] = h
-        table[3 * short : 4 * short, cut] = jnp.zeros_like(h)
+    wave_columns(slot_ref, wave_own)
+    single_table(wave_own[pl.ds(slots - 1, devices, stride=slots), :], table, longitudes)
     pull.wait()
-    flat = pulled.reshape(devices * each, lats)
-
-    def gather(l, carry):
-        x = jnp.concatenate(
-            [flat[pl.ds(c * levels + l, devices, stride=each), :] for c in range(2)], axis=0
-        )
-        turned[pl.ds(l, lats, stride=levels), :] = jnp.concatenate([x, x], axis=0).T
-        return carry
-
-    lax.fori_loop(0, levels, gather, 0)
-    keep = lax.broadcasted_iota(jnp.int32, (levels, LANES), 1) < short
-
-    def split(r, carry):
-        lat = jnp.where(south, lats - 1 - r, r)
-        h, l = halves_of(turned[aligned(lat * levels, levels), :])
-        to = aligned(r * levels, levels)
-        stacked[to, 0:LANES] = h
-        stacked[to, LANES : 2 * LANES] = jnp.where(keep, l, jnp.zeros_like(l))
-        return carry
-
-    lax.fori_loop(0, lats, split, 0)
+    single_rows(dims, south, pulled.reshape(devices * each, lats), turned, 0, stacked)
 
     def outer(m, carry):
         slot = lax.rem(m, 2)
@@ -600,8 +702,8 @@
     spec_copy.wait()
     done = pltpu.make_async_copy(spec, spec_out, spec_done)
     done.start()
-    lax.fori_loop(0, PIECES, outer, 0)
-    for m in range(PIECES - 2, PIECES):
+    lax.fori_loop(0, BLOCKS, outer, 0)
+    for m in range(BLOCKS - 2, BLOCKS):
         out_copy(m, m % 2).wait()
     done.wait()
 
@@ -620,7 +722,7 @@
         lats == LANES and levels == 2 * SUB and 4 * devices == LANES
         and longitudes % (2 * LANES) == 0 and longitudes & (longitudes - 1) == 0
         and bands % 2 == 0 and half == bands // 2 * lats and depth % LANES == 0
-        and slots % GROUP == 0 and 2 * every == LANES and to_modes.shape[0] == every
+        and slots % GROUP == 0 and devices * slots % LANES == 0 and levels // PAIR >= 3 and 2 * every == LANES and to_modes.shape[0] == every
     )
     if not fits:
         return plain_shards(
@@ -629,16 +731,12 @@
         )
     dims = (bands, parts, lats, levels, longitudes, slots, depth, half)
     count = devices * slots * 2
-    waves = slot_wavenumber.reshape(devices, slots // GROUP, GROUP).transpose(1, 0, 2)
-    waves = jnp.broadcast_to(waves[:, :, :, None, None], waves.shape + (2, LANES))
-    waves = waves.reshape(count, LANES)
-    rate = jnp.broadcast_to(rates[None, :, None], (2, every, LANES)).reshape(2 * every, LANES)
-
     hbm = pl.BlockSpec(memory_space=pl.ANY)
     vmem = pl.BlockSpec(memory_space=pltpu.VMEM)
     f32, bf16 = jnp.float32, jnp.bfloat16
     dma = pltpu.SemaphoreType.DMA
     wide = longitudes // LANES
+    numbers = slot_wavenumber.reshape(-1, LANES)
     state = spectral_state.transpose(0, 2, 3, 1).reshape(slots, 2 * every, depth)
     square = pltpu.VMEM((2 * every, 2 * every), f32)
     spectral, returned, partial = pl.pallas_call(
@@ -666,15 +764,21 @@
             square, square, square,
             pltpu.VMEM((lats * levels, devices * 2 * GROUP), bf16),
             pltpu.VMEM((lats * levels, devices * 2 * GROUP), bf16),
-            dma((2,)), dma((2,)), dma, dma, dma, dma((slots // GROUP + 1,)),
+            pltpu.VMEM((devices * slots, LANES), jnp.int32),
+            pltpu.VMEM((count, LANES), jnp.int32),
+            square,
+            pltpu.VMEM((2 * LANES, longitudes), bf16),
+            dma((2,)), dma((2,)), dma, dma((slots // GROUP + 1,)), dma,
+            dma((slots // GROUP - 1 + GROUP,)),
             dma((2,)), dma((2,)), dma((2,)), dma,
         ],
         compiler_params=pltpu.CompilerParams(
-            collective_id=0, has_side_effects=True, vmem_limit_bytes=KEEP
+            collective_id=0, has_side_effects=True, vmem_limit_bytes=GRANT
         ),
         name="spectral",
     )(
-        grid_adjoint, trajectory, waves, legendre_north, state, rate, to_modes, from_modes,
+        grid_adjoint, trajectory, numbers, legendre_north, state, rates.reshape(1, every),
+        to_modes, from_modes,
     )
     grid, spectral = pl.pallas_call(
         functools.partial(finish_kernel, dims),
@@ -689,13 +793,14 @@
             pltpu.VMEM((lats * levels, LANES), f32),
             pltpu.VMEM((lats * levels, 2 * LANES), bf16),
             pltpu.VMEM((2 * LANES, longitudes), bf16),
-            pltpu.VMEM((2, lats // PIECES, levels, longitudes), f32),
+            pltpu.VMEM((2, lats // BLOCKS, levels, longitudes), f32),
             pltpu.VMEM(spectral.shape, f32),
+            pltpu.VMEM((devices * slots, LANES), jnp.int32),
             dma, dma((2,)), dma, dma,
         ],
-        compiler_params=pltpu.CompilerParams(vmem_limit_bytes=KEEP),
+        compiler_params=pltpu.CompilerParams(vmem_limit_bytes=LAST_GRANT),
         name="finish",
-    )(returned, partial, spectral, waves)
+    )(returned, pltpu.with_memory_space_constraint(partial, pltpu.VMEM), spectral, numbers)
     return spectral.reshape(slots, 2, every, depth).transpose(0, 3, 1, 2), grid
 
 

time: 435 us -> 415 us (0.954)
  local copies, waits for them, and re-layouts: 11.6 us -> 0 us
  Pallas kernels: 422 us -> 414 us
    pallas_call x1, Pallas kernels: 24.6 us -> 15.5 us  [shards(): pl.pallas_call(functools.partial(finish_kernel, dims), out_shape=(jax.Sha...]
    unnamed x6 -> x0, local copies, waits for them, and re-layouts: 7.91 us -> none
where the time goes in v4:
time: 415 us
  Pallas kernels  414 us (100%)
    pallas_call x1, Pallas kernels, shards(): pl.pallas_call(functools.partial(forward_kernel, dims), out_shape=(jax.Sh...  399 us
    pallas_call x1, Pallas kernels, shards(): pl.pallas_call(functools.partial(finish_kernel, dims), out_shape=(jax.Sha...  15.5 us

profile of v4, /device:TPU:0, one launch (start us, length us, event | category | flops | bytes accessed | tf_op | source)
XLA Modules:
  0.0 414.7 jit_solution(1580641033309249839)
XLA Ops:
  0.6 398.6 %spectral.1 = (f32[16,128,512]{2,1,0:T(8,128)}, f32[32,512,128]{2,1,0:T(8,128)}, f32[16,2048,128]{2,1,0:T(8,128)S(1)}) custom-call(f32[128,16,2048]{2,1,0:T(8,128)} %grid_ref.1, f32[128,16,2048]{2,1,0:T(8,128)} %traj_ref.1, s32[4,128]{1,0:T(4,128)} %bitcast.9, f32[16,512,512]{2,1,0:T(8,128)} %leg_ref.1, f32[16,128,512]{2,1,0:T(8,128)} %bitcast.8, ...), custom_call_target="tpu_custom_call" | custom-call | tf_op jit(solution)/shard_map/spectral/pallas_call | solution.py:742
  399.2 15.5 %finish.1 = (f32[128,16,2048]{2,1,0:T(8,128)}, f32[16,128,512]{2,1,0:T(8,128)}) custom-call(f32[32,512,128]{2,1,0:T(8,128)} %get-tuple-element.7.returned, f32[16,2048,128]{2,1,0:T(8,128)S(1)} %get-tuple-element.8.partial, f32[16,128,512]{2,1,0:T(8,128)} %get-tuple-element.9.spectral, s32[4,128]{1,0:T(4,128)} %bitcast.10), custom_call_target="tpu_custom_call" | custom-call | tf_op jit(solution)/shard_map/finish/pallas_call | solution.py:783

commit v5 on v4

--- a/solution.py
+++ b/solution.py
@@ -181,42 +181,43 @@
         own[i * LANES : (i + 1) * LANES, :] = row.T.astype(jnp.int32)
 
 
-def single_table(waves, table, longitudes):
-    devices = waves.shape[0]
-    waves = jnp.concatenate([waves, waves], axis=0)
-    imaginary = lax.broadcasted_iota(jnp.int32, waves.shape, 0) >= devices
-    short = 2 * devices
-    for i, (h, l) in enumerate(table_rows(waves, imaginary, longitudes)):
-        cut = slice(i * LANES, (i + 1) * LANES)
-        table[0:short, cut] = h
-        table[short : 2 * short, cut] = l
-        table[2 * short : 3 * short, cut] = h
-        table[3 * short : 4 * short, cut] = jnp.zeros_like(h)
-
-
-def single_rows(dims, south, flat, turned, base, stacked):
+def last_rows(dims, south, flat, turned, stacked):
     bands, parts, lats, levels = dims[:4]
-    devices = bands * parts
 
     def gather(l, carry):
-        x = jnp.concatenate(
-            [flat[pl.ds(c * levels + l, devices, stride=2 * levels), :] for c in range(2)], axis=0
-        )
-        turned[pl.ds(base + l, lats, stride=levels), :] = jnp.concatenate([x, x], axis=0).T
+        x = flat[pl.ds(l, LANES // 2, stride=levels), :]
+        turned[pl.ds(l, lats, stride=levels), :] = jnp.concatenate([x, x], axis=0).T
         return carry
 
     lax.fori_loop(0, levels, gather, 0)
-    keep = lax.broadcasted_iota(jnp.int32, (levels, LANES), 1) < 2 * devices
+    keep = lax.broadcasted_iota(jnp.int32, (levels, LANES), 1) < LANES // 2
 
     def split(r, carry):
         lat = jnp.where(south, lats - 1 - r, r)
-        h, l = halves_of(turned[aligned(base + lat * levels, levels), :])
+        h, l = halves_of(turned[aligned(lat * levels, levels), :])
         to = aligned(r * levels, levels)
         stacked[to, 0:LANES] = h
         stacked[to, LANES : 2 * LANES] = jnp.where(keep, l, jnp.zeros_like(l))
         return carry
 
     lax.fori_loop(0, lats, split, 0)
+
+
+def senders(quarter):
+    return (
+        quarter,
+        jnp.bitwise_xor(quarter, 1),
+        jnp.where(quarter < 2, 3, 0),
+        jnp.where(quarter < 2, 2, 1),
+    )
+
+
+ARRIVALS = (
+    ((1, 0), (1, 1), (2, 0), (3, 0)),
+    ((0, 0), (0, 1), (0, 2), (2, 1)),
+    ((1, 2), (1, 3), (2, 2), (2, 3)),
+    ((0, 3), (3, 1), (3, 2)),
+)
 
 
 def forward_kernel(
@@ -224,7 +225,7 @@
     grid_ref, traj_ref, slot_ref, leg_ref, state_ref, rate_ref, to_ref, from_ref,
     spec_out, returned, forced,
     high, low, stage, traj, rows_h, rows_l, sending, arrived, synth, leg, state, spec,
-    into, outof, back, flat_h, flat_l, wave_own, wave_ref, rate_col, single,
+    into, outof, back, flat_h, flat_l, wave_own, wave_ref, rate_col,
     grid_sem, traj_sem, send_sem, recv_sem, send2_sem, recv2_sem, leg_sem, state_sem, spec_sem,
     pull_sem,
 ):
@@ -458,7 +459,8 @@
     even = lax.rem(lane, 2) == 0
     folds = bands // 2
     each = 2 * levels
-    whole = slots - GROUP
+    quarter = devices // 4
+    order = senders(me // quarter)
 
     def column(b, s):
         return jnp.concatenate(
@@ -481,7 +483,7 @@
 
     def one_slot(s, carry):
         slot = lax.rem(s, 2)
-        sem = jnp.where(s < whole, s // GROUP, groups - 1 + s - whole)
+        sem = me // quarter * groups + s // GROUP
 
         @pl.when(lax.rem(s, GROUP) == 0)
         def _():
@@ -549,20 +551,33 @@
 
     lax.fori_loop(0, slots, one_slot, 0)
 
-    staged = devices * GROUP * each
-    pulled = arrived.reshape(levels * count_rows // (GROUP * each), GROUP * each, lats)
+    rows = GROUP * each
+    staged = devices * rows
+    pulled = arrived.reshape(levels * count_rows // rows, rows, lats)
     block = 1024
-
-    for g in range(groups - 1):
-        rows = GROUP * each
-        here = returned.at[:, g * rows : (g + 1) * rows, :]
-        pltpu.make_async_copy(here, here, recv2_sem.at[g]).wait()
-        copy = pltpu.make_async_copy(here, pulled.at[0:devices, 0:rows, :], pull_sem)
-        copy.start()
-        copy.wait()
+    piece = quarter * small
+
+    def landed(c, g):
+        return returned.at[aligned(order[c] * quarter, quarter), g * rows : (g + 1) * rows, :]
+
+    for number, units in enumerate(ARRIVALS):
+        copies = []
+        for u, (c, g) in enumerate(units):
+            here = landed(c, g)
+            pltpu.make_async_copy(here, here, recv2_sem.at[order[c] * groups + g]).wait()
+            copy = pltpu.make_async_copy(
+                here, pulled.at[u * quarter : (u + 1) * quarter], pull_sem.at[u]
+            )
+            copy.start()
+            copies.append(copy)
+        for copy in copies:
+            copy.wait()
+        filled = len(units) * piece
 
         def pull(l, carry):
             x = arrived[pl.ds(l, tall, stride=levels), :]
+            if filled < tall:
+                x = jnp.where(lax.broadcasted_iota(jnp.int32, x.shape, 0) < filled, x, 0.0)
             x = x.T
             for j in range(tall // LANES):
                 arrived[pl.ds(staged + j * lats * levels + l, lats, stride=levels), :] = x[
@@ -583,58 +598,32 @@
             return carry
 
         lax.fori_loop(0, lats, split, 0)
+        chosen = (units + units[:1])[: tall // piece]
 
         def multiply(m, carry):
             at = aligned(m * block, block)
 
-            def inner(w, c):
+            def inner(w, carry2):
                 cut = aligned(w * 2 * LANES, 2 * LANES)
-                rows_at = slice(g * tall, (g + 1) * tall)
-                got = dot3(
-                    (flat_h[at, :], flat_l[at, :]), (high[rows_at, cut], low[rows_at, cut]), NN
-                )
+                table = [
+                    jnp.concatenate(
+                        [part[aligned(g * tall + order[c] * piece, piece), cut] for c, g in chosen],
+                        axis=0,
+                    )
+                    for part in (high, low)
+                ]
+                got = dot3((flat_h[at, :], flat_l[at, :]), table, NN)
                 for j in range(2):
                     x = got[:, j * LANES : (j + 1) * LANES]
-                    if g > 0:
+                    if number > 0:
                         x = x + forced[2 * w + j, at, :]
                     forced[2 * w + j, at, :] = x
-                return c
+                return carry2
 
             lax.fori_loop(0, wide // 2, inner, 0)
             return carry
 
         lax.fori_loop(0, lats * levels // block, multiply, 0)
-
-    thin = arrived.reshape(levels * count_rows // each, each, lats)
-
-    def lone(i, carry):
-        s = whole + i
-        single_table(wave_own[pl.ds(s, devices, stride=slots), :], single, longitudes)
-        here = returned.at[:, aligned(s * each, each), :]
-        pltpu.make_async_copy(here, here, recv2_sem.at[groups - 1 + i]).wait()
-        copy = pltpu.make_async_copy(here, thin.at[0:devices], pull_sem)
-        copy.start()
-        copy.wait()
-        single_rows(dims, south, arrived, arrived, staged, flat_h)
-
-        def multiply(m, carry):
-            at = aligned(m * block, block)
-
-            def inner(w, c):
-                got = dot1(flat_h[at, :], single[:, aligned(w * 2 * LANES, 2 * LANES)], NN)
-                for j in range(2):
-                    forced[2 * w + j, at, :] = (
-                        forced[2 * w + j, at, :] + got[:, j * LANES : (j + 1) * LANES]
-                    )
-                return c
-
-            lax.fori_loop(0, wide // 2, inner, 0)
-            return carry
-
-        lax.fori_loop(0, lats * levels // block, multiply, 0)
-        return carry
-
-    lax.fori_loop(0, GROUP - 1, lone, 0)
 
     for s in range(max(slots - 2, 0), slots):
         pltpu.make_async_copy(spec.at[s % 2], spec_out.at[s], spec_sem.at[s % 2]).wait()
@@ -642,13 +631,13 @@
     pltpu.make_async_copy(sending.at[sent, :], sending.at[sent, :], send_sem).wait()
     sent = pl.ds(0, slots * (devices - 1) * each)
     pltpu.make_async_copy(synth.at[sent, :], synth.at[sent, :], send2_sem).wait()
-    final = returned.at[:, (slots - 1) * each : slots * each, :]
-    pltpu.make_async_copy(final, final, recv2_sem.at[groups - 1 + GROUP - 1]).wait()
+    final = landed(3, groups - 1)
+    pltpu.make_async_copy(final, final, recv2_sem.at[order[3] * groups + groups - 1]).wait()
 
 
 def finish_kernel(
     dims, returned, partial, spectral, slot_ref, grid_out, spec_out,
-    pulled, turned, stacked, table, result, spec, wave_own,
+    pulled, turned, stacked, table, result, spec, wave_own, waves,
     pull_sem, out_sem, spec_in, spec_done,
 ):
     bands, parts, lats, levels, longitudes, slots, depth, half = dims
@@ -664,17 +653,32 @@
             result.at[slot], grid_out.at[aligned(m * span, span), :, :], out_sem.at[slot]
         )
 
+    quarter = devices // 4
+    me = lax.axis_index("band") * parts + lax.axis_index("lev")
+    first = senders(me // quarter)[3] * quarter
+    rows = GROUP * each
     pull = pltpu.make_async_copy(
-        returned.at[:, (slots - 1) * each : slots * each, :], pulled, pull_sem
+        returned.at[aligned(first, quarter), slots * each - rows : slots * each, :], pulled, pull_sem
     )
     pull.start()
     spec_copy = pltpu.make_async_copy(spectral, spec, spec_in)
     spec_copy.start()
 
     wave_columns(slot_ref, wave_own)
-    single_table(wave_own[pl.ds(slots - 1, devices, stride=slots), :], table, longitudes)
+    for i in range(GROUP):
+        x = wave_own[pl.ds(first * slots + slots - GROUP + i, quarter, stride=slots), :]
+        for c in range(2):
+            waves[pl.ds(2 * i + c, quarter, stride=2 * GROUP), :] = x
+    imaginary = (lax.broadcasted_iota(jnp.int32, waves.shape, 0) & 1) == 1
+    short = quarter * 2 * GROUP
+    for i, (h, l) in enumerate(table_rows(waves[...], imaginary, longitudes)):
+        cut = slice(i * LANES, (i + 1) * LANES)
+        table[0:short, cut] = h
+        table[short : 2 * short, cut] = l
+        table[2 * short : 3 * short, cut] = h
+        table[3 * short : 4 * short, cut] = jnp.zeros_like(h)
     pull.wait()
-    single_rows(dims, south, pulled.reshape(devices * each, lats), turned, 0, stacked)
+    last_rows(dims, south, pulled.reshape(quarter * rows, lats), turned, stacked)
 
     def outer(m, carry):
         slot = lax.rem(m, 2)
@@ -722,7 +726,7 @@
         lats == LANES and levels == 2 * SUB and 4 * devices == LANES
         and longitudes % (2 * LANES) == 0 and longitudes & (longitudes - 1) == 0
         and bands % 2 == 0 and half == bands // 2 * lats and depth % LANES == 0
-        and slots % GROUP == 0 and devices * slots % LANES == 0 and levels // PAIR >= 3 and 2 * every == LANES and to_modes.shape[0] == every
+        and slots == 4 * GROUP and devices * slots % LANES == 0 and levels // PAIR >= 3 and 2 * every == LANES and to_modes.shape[0] == every
     )
     if not fits:
         return plain_shards(
@@ -767,10 +771,9 @@
             pltpu.VMEM((devices * slots, LANES), jnp.int32),
             pltpu.VMEM((count, LANES), jnp.int32),
             square,
-            pltpu.VMEM((2 * LANES, longitudes), bf16),
             dma((2,)), dma((2,)), dma, dma((slots // GROUP + 1,)), dma,
-            dma((slots // GROUP - 1 + GROUP,)),
-            dma((2,)), dma((2,)), dma((2,)), dma,
+            dma((slots,)),
+            dma((2,)), dma((2,)), dma((2,)), dma((4,)),
         ],
         compiler_params=pltpu.CompilerParams(
             collective_id=0, has_side_effects=True, vmem_limit_bytes=GRANT
@@ -789,13 +792,14 @@
         in_specs=[hbm, vmem, hbm, vmem],
         out_specs=(hbm, hbm),
         scratch_shapes=[
-            pltpu.VMEM((devices, 2 * levels, lats), f32),
+            pltpu.VMEM((devices // 4, GROUP * 2 * levels, lats), f32),
             pltpu.VMEM((lats * levels, LANES), f32),
             pltpu.VMEM((lats * levels, 2 * LANES), bf16),
             pltpu.VMEM((2 * LANES, longitudes), bf16),
             pltpu.VMEM((2, lats // BLOCKS, levels, longitudes), f32),
             pltpu.VMEM(spectral.shape, f32),
             pltpu.VMEM((devices * slots, LANES), jnp.int32),
+            pltpu.VMEM((LANES // 2, LANES), jnp.int32),
             dma, dma((2,)), dma, dma,
         ],
         compiler_params=pltpu.CompilerParams(vmem_limit_bytes=LAST_GRANT),

time: 415 us -> 396 us (0.954)
  Pallas kernels: 414 us -> 395 us
    pallas_call x1, Pallas kernels: 399 us -> 378 us  [shards(): pl.pallas_call(functools.partial(forward_kernel, dims), out_shape=(jax.Sh...]
where the time goes in v5:
time: 396 us; the launch traced here: 395 us
  Pallas kernels  395 us (100%)
    pallas_call x1, Pallas kernels, shards(): pl.pallas_call(functools.partial(forward_kernel, dims), out_shape=(jax.Sh...  378 us
    pallas_call x1, Pallas kernels, shards(): pl.pallas_call(functools.partial(finish_kernel, dims), out_shape=(jax.Sha...  16.7 us

profile of v5, /device:TPU:0, one launch (start us, length us, event | category | flops | bytes accessed | tf_op | source)
XLA Modules:
  0.0 395.3 jit_solution(11799048174451097550)
XLA Ops:
  0.6 378.0 %spectral.1 = (f32[16,128,512]{2,1,0:T(8,128)}, f32[32,512,128]{2,1,0:T(8,128)}, f32[16,2048,128]{2,1,0:T(8,128)S(1)}) custom-call(f32[128,16,2048]{2,1,0:T(8,128)} %grid_ref.1, f32[128,16,2048]{2,1,0:T(8,128)} %traj_ref.1, s32[4,128]{1,0:T(4,128)} %bitcast.9, f32[16,512,512]{2,1,0:T(8,128)} %leg_ref.1, f32[16,128,512]{2,1,0:T(8,128)} %bitcast.8, ...), custom_call_target="tpu_custom_call" | custom-call | tf_op jit(solution)/shard_map/spectral/pallas_call | solution.py:746
  378.6 16.7 %finish.1 = (f32[128,16,2048]{2,1,0:T(8,128)}, f32[16,128,512]{2,1,0:T(8,128)}) custom-call(f32[32,512,128]{2,1,0:T(8,128)} %get-tuple-element.7.returned, f32[16,2048,128]{2,1,0:T(8,128)S(1)} %get-tuple-element.8.partial, f32[16,128,512]{2,1,0:T(8,128)} %get-tuple-element.9.spectral, s32[4,128]{1,0:T(4,128)} %bitcast.10), custom_call_target="tpu_custom_call" | custom-call | tf_op jit(solution)/shard_map/finish/pallas_call | solution.py:786

commit v6 on v5

--- a/solution.py
+++ b/solution.py
@@ -114,7 +114,6 @@
 PAIR = 2
 PIECES = 8
 GROUP = 4
-BLOCKS = 4
 GRANT = 50_000_000
 LAST_GRANT = 44_000_000
 NN = (((1,), (0,)), ((), ()))
@@ -181,28 +180,6 @@
         own[i * LANES : (i + 1) * LANES, :] = row.T.astype(jnp.int32)
 
 
-def last_rows(dims, south, flat, turned, stacked):
-    bands, parts, lats, levels = dims[:4]
-
-    def gather(l, carry):
-        x = flat[pl.ds(l, LANES // 2, stride=levels), :]
-        turned[pl.ds(l, lats, stride=levels), :] = jnp.concatenate([x, x], axis=0).T
-        return carry
-
-    lax.fori_loop(0, levels, gather, 0)
-    keep = lax.broadcasted_iota(jnp.int32, (levels, LANES), 1) < LANES // 2
-
-    def split(r, carry):
-        lat = jnp.where(south, lats - 1 - r, r)
-        h, l = halves_of(turned[aligned(lat * levels, levels), :])
-        to = aligned(r * levels, levels)
-        stacked[to, 0:LANES] = h
-        stacked[to, LANES : 2 * LANES] = jnp.where(keep, l, jnp.zeros_like(l))
-        return carry
-
-    lax.fori_loop(0, lats, split, 0)
-
-
 def senders(quarter):
     return (
         quarter,
@@ -222,12 +199,13 @@
 
 def forward_kernel(
     dims,
-    grid_ref, traj_ref, slot_ref, leg_ref, state_ref, rate_ref, to_ref, from_ref,
+    grid_ref, traj_ref, slot_in, leg_ref, state_ref, rate_in, to_in, from_in,
     spec_out, returned, forced,
     high, low, stage, traj, rows_h, rows_l, sending, arrived, synth, leg, state, spec,
     into, outof, back, flat_h, flat_l, wave_own, wave_ref, rate_col,
+    slot_ref, rate_ref, to_ref, from_ref,
     grid_sem, traj_sem, send_sem, recv_sem, send2_sem, recv2_sem, leg_sem, state_sem, spec_sem,
-    pull_sem,
+    pull_sem, tiny_sem,
 ):
     bands, parts, lats, levels, longitudes, slots, depth, half = dims
     devices = bands * parts
@@ -247,6 +225,14 @@
     def mesh_id(d):
         return (d // parts, lax.rem(d, parts))
 
+    tiny = [
+        pltpu.make_async_copy(source, target, tiny_sem.at[i])
+        for i, (source, target) in enumerate(
+            ((slot_in, slot_ref), (rate_in, rate_ref), (to_in, to_ref), (from_in, from_ref))
+        )
+    ]
+    for copy in tiny:
+        copy.start()
     barrier = pltpu.get_barrier_semaphore()
 
     def greet(i, carry):
@@ -256,7 +242,6 @@
         )
         return carry
 
-    lax.fori_loop(1, devices, greet, 0)
 
     span = lats // PIECES
     count = (levels // SUB) * PIECES
@@ -298,6 +283,7 @@
 
     load_piece(jnp.int32(0))
     load_piece(jnp.int32(1))
+    lax.fori_loop(1, devices, greet, 0)
 
     def leg_copy(s, slot):
         return pltpu.make_async_copy(leg_ref.at[s], leg.at[slot], leg_sem.at[slot])
@@ -305,14 +291,13 @@
     def state_copy(s, slot):
         return pltpu.make_async_copy(state_ref.at[s], state.at[slot], state_sem.at[slot])
 
+    tiny[0].wait()
     wave_columns(slot_ref, wave_own)
     for g in range(groups):
         for i in range(GROUP):
             x = wave_own[pl.ds(g * GROUP + i, devices, stride=slots), :]
             for c in range(2):
                 wave_ref[pl.ds(g * tall + 2 * i + c, devices, stride=small), :] = x
-    rate = jnp.concatenate([rate_ref[...], rate_ref[...]], axis=1)
-    rate_col[...] = jnp.broadcast_to(rate, (2 * every, 2 * every)).T
     block_rows = 64
 
     def fill(r, carry):
@@ -399,11 +384,20 @@
         finish_piece(i)
         return c
 
-    lax.fori_loop(0, PIECES, finish, 0)
+    fills = devices * unit // block_rows // PIECES // 2
+
+    def begin(i, c):
+        lax.fori_loop(i * fills, (i + 1) * fills, fill, 0)
+        return finish(i, c)
+
+    lax.fori_loop(0, PIECES, begin, 0)
     extract(jnp.int32(0))
 
     def opening(r, carry):
-        lax.fori_loop(r * (tall // block_rows), (r + 1) * (tall // block_rows), fill, 0)
+        @pl.when(r >= groups // 2)
+        def _():
+            lax.fori_loop(r * (tall // block_rows), (r + 1) * (tall // block_rows), fill, 0)
+
         transform(0, r)
 
         @pl.when(r == 0)
@@ -439,6 +433,10 @@
         return carry
 
     lax.fori_loop(0, groups, closing, 0)
+    for copy in tiny[1:]:
+        copy.wait()
+    rate = jnp.concatenate([rate_ref[...], rate_ref[...]], axis=1)
+    rate_col[...] = jnp.broadcast_to(rate, (2 * every, 2 * every)).T
     for m in (into, outof, back):
         m[...] = jnp.zeros_like(m)
     for c in range(2):
@@ -645,12 +643,14 @@
     each = 2 * levels
     wide = longitudes // LANES
     south = lax.axis_index("band") >= bands // 2
-    span = lats // BLOCKS
-    block = span * levels
-
-    def out_copy(m, slot):
+    block = 1024
+    span = block // levels
+
+    def out_copy(w, slot):
         return pltpu.make_async_copy(
-            result.at[slot], grid_out.at[aligned(m * span, span), :, :], out_sem.at[slot]
+            result.at[slot],
+            grid_out.at[:, :, aligned(w * 2 * LANES, 2 * LANES)],
+            out_sem.at[slot],
         )
 
     quarter = devices // 4
@@ -677,38 +677,53 @@
         table[short : 2 * short, cut] = l
         table[2 * short : 3 * short, cut] = h
         table[3 * short : 4 * short, cut] = jnp.zeros_like(h)
-    pull.wait()
-    last_rows(dims, south, pulled.reshape(quarter * rows, lats), turned, stacked)
-
-    def outer(m, carry):
-        slot = lax.rem(m, 2)
-        @pl.when(m >= 2)
-        def _():
-            out_copy(m - 2, slot).wait()
-
-        at = aligned(m * block, block)
-        a = stacked[at, :]
-
-        def inner(w, c):
-            cut = aligned(w * 2 * LANES, 2 * LANES)
-            got = dot1(a, table[:, cut], NN)
-            for j in range(2):
-                x = got[:, j * LANES : (j + 1) * LANES] + partial[2 * w + j, at, :]
-                to = aligned((2 * w + j) * LANES, LANES)
-                result[slot, :, :, to] = x.reshape(span, levels, LANES)
-            return c
-
-        lax.fori_loop(0, wide // 2, inner, 0)
-        out_copy(m, slot).start()
-
-        return carry
-
     spec_copy.wait()
     done = pltpu.make_async_copy(spec, spec_out, spec_done)
     done.start()
-    lax.fori_loop(0, BLOCKS, outer, 0)
-    for m in range(BLOCKS - 2, BLOCKS):
-        out_copy(m, m % 2).wait()
+    pull.wait()
+    flat = pulled.reshape(quarter * rows, lats)
+    for l in range(levels):
+        x = flat[pl.ds(l, LANES // 2, stride=levels), :]
+        turned[pl.ds(l, lats, stride=levels), :] = jnp.concatenate([x, x], axis=0).T
+    keep = lax.broadcasted_iota(jnp.int32, (levels, LANES), 1) < LANES // 2
+
+    burst = 8
+
+    def split(i, carry):
+        for e in range(burst):
+            r = i * burst + e
+            lat = jnp.where(south, lats - 1 - r, r)
+            h, l = halves_of(turned[aligned(lat * levels, levels), :])
+            to = aligned(r * levels, levels)
+            stacked[to, 0:LANES] = h
+            stacked[to, LANES : 2 * LANES] = jnp.where(keep, l, jnp.zeros_like(l))
+        return carry
+
+    lax.fori_loop(0, lats // burst, split, 0)
+
+    def outer(w, carry):
+        slot = lax.rem(w, 2)
+
+        @pl.when(w >= 2)
+        def _():
+            out_copy(w - 2, slot).wait()
+
+        cut = aligned(w * 2 * LANES, 2 * LANES)
+        for m in range(lats // span):
+            at = slice(m * block, (m + 1) * block)
+            got = dot1(stacked[at, :], table[:, cut], NN)
+            for j in range(2):
+                x = got[:, j * LANES : (j + 1) * LANES] + partial[2 * w + j, at, :]
+                result[slot, m * span : (m + 1) * span, :, j * LANES : (j + 1) * LANES] = (
+                    x.reshape(span, levels, LANES)
+                )
+        out_copy(w, slot).start()
+        return carry
+
+    turns = wide // 2
+    lax.fori_loop(0, turns, outer, 0)
+    for w in range(turns - 2, turns):
+        out_copy(w, w % 2).wait()
     done.wait()
 
 
@@ -750,7 +765,7 @@
             jax.ShapeDtypeStruct((devices, slots * 2 * levels, lats), f32),
             pltpu.VMEM((wide, lats * levels, LANES), f32),
         ),
-        in_specs=[hbm, hbm, vmem, hbm, hbm, vmem, vmem, vmem],
+        in_specs=[hbm] * 8,
         out_specs=(hbm, hbm, vmem),
         scratch_shapes=[
             pltpu.VMEM((count, longitudes), bf16),
@@ -771,9 +786,13 @@
             pltpu.VMEM((devices * slots, LANES), jnp.int32),
             pltpu.VMEM((count, LANES), jnp.int32),
             square,
+            pltpu.VMEM(numbers.shape, jnp.int32),
+            pltpu.VMEM((1, every), f32),
+            pltpu.VMEM(to_modes.shape, f32),
+            pltpu.VMEM(from_modes.shape, f32),
             dma((2,)), dma((2,)), dma, dma((slots // GROUP + 1,)), dma,
             dma((slots,)),
-            dma((2,)), dma((2,)), dma((2,)), dma((4,)),
+            dma((2,)), dma((2,)), dma((2,)), dma((4,)), dma((4,)),
         ],
         compiler_params=pltpu.CompilerParams(
             collective_id=0, has_side_effects=True, vmem_limit_bytes=GRANT
@@ -796,7 +815,7 @@
             pltpu.VMEM((lats * levels, LANES), f32),
             pltpu.VMEM((lats * levels, 2 * LANES), bf16),
             pltpu.VMEM((2 * LANES, longitudes), bf16),
-            pltpu.VMEM((2, lats // BLOCKS, levels, longitudes), f32),
+            pltpu.VMEM((2, lats, levels, 2 * LANES), f32),
             pltpu.VMEM(spectral.shape, f32),
             pltpu.VMEM((devices * slots, LANES), jnp.int32),
             pltpu.VMEM((LANES // 2, LANES), jnp.int32),

time: 396 us -> 388 us (0.980)
  Pallas kernels: 395 us -> 387 us
    pallas_call x1, Pallas kernels: 16.7 us -> 11.6 us  [shards(): pl.pallas_call(functools.partial(finish_kernel, dims), out_shape=(jax.Sha...]
where the time goes in v6:
time: 388 us
  Pallas kernels  387 us (100%)
    pallas_call x1, Pallas kernels, shards(): pl.pallas_call(functools.partial(forward_kernel, dims), out_shape=(jax.Sh...  375 us
    pallas_call x1, Pallas kernels, shards(): pl.pallas_call(functools.partial(finish_kernel, dims), out_shape=(jax.Sha...  11.6 us

profile of v6, /device:TPU:0, one launch (start us, length us, event | category | flops | bytes accessed | tf_op | source)
XLA Modules:
  0.0 387.6 jit_solution(5415783620697291003)
XLA Ops:
  0.6 375.4 %spectral.1 = (f32[16,128,512]{2,1,0:T(8,128)}, f32[32,512,128]{2,1,0:T(8,128)}, f32[16,2048,128]{2,1,0:T(8,128)S(1)}) custom-call(f32[128,16,2048]{2,1,0:T(8,128)} %grid_ref.1, f32[128,16,2048]{2,1,0:T(8,128)} %traj_ref.1, s32[4,128]{1,0:T(4,128)} %bitcast.9, f32[16,512,512]{2,1,0:T(8,128)} %leg_ref.1, f32[16,128,512]{2,1,0:T(8,128)} %bitcast.8, ...), custom_call_target="tpu_custom_call" | custom-call | tf_op jit(solution)/shard_map/spectral/pallas_call | solution.py:761
  376.0 11.6 %finish.1 = (f32[128,16,2048]{2,1,0:T(8,128)}, f32[16,128,512]{2,1,0:T(8,128)}) custom-call(f32[32,512,128]{2,1,0:T(8,128)} %get-tuple-element.7.returned, f32[16,2048,128]{2,1,0:T(8,128)S(1)} %get-tuple-element.8.partial, f32[16,128,512]{2,1,0:T(8,128)} %get-tuple-element.9.spectral, s32[4,128]{1,0:T(4,128)} %bitcast.10), custom_call_target="tpu_custom_call" | custom-call | tf_op jit(solution)/shard_map/finish/pallas_call | solution.py:805

commit v7 on v6

--- a/solution.py
+++ b/solution.py
@@ -114,8 +114,8 @@
 PAIR = 2
 PIECES = 8
 GROUP = 4
-GRANT = 50_000_000
-LAST_GRANT = 44_000_000
+GRANT = 47_000_000
+LAST_GRANT = 43_000_000
 NN = (((1,), (0,)), ((), ()))
 NT = (((1,), (1,)), ((), ()))
 
@@ -201,7 +201,7 @@
     dims,
     grid_ref, traj_ref, slot_in, leg_ref, state_ref, rate_in, to_in, from_in,
     spec_out, returned, forced,
-    high, low, stage, traj, rows_h, rows_l, sending, arrived, synth, leg, state, spec,
+    high, low, stage, traj, rows_h, rows_l, outbox, arrived, leg, state, spec,
     into, outof, back, flat_h, flat_l, wave_own, wave_ref, rate_col,
     slot_ref, rate_ref, to_ref, from_ref,
     grid_sem, traj_sem, send_sem, recv_sem, send2_sem, recv2_sem, leg_sem, state_sem, spec_sem,
@@ -215,6 +215,7 @@
     message = PAIR * unit
     small = 2 * GROUP
     tall = devices * small
+    ahead = slots // 2 * devices * 2 * levels
     groups = slots // GROUP
     count_rows = devices * unit
     wide = longitudes // LANES
@@ -311,7 +312,7 @@
 
     def greeted_copy(source, target, d, sem):
         return pltpu.make_async_remote_copy(
-            src_ref=sending.at[source, :],
+            src_ref=outbox.at[source, :],
             dst_ref=arrived.at[target, :],
             send_sem=send_sem,
             recv_sem=recv_sem.at[sem],
@@ -327,32 +328,33 @@
 
         def body(i, carry):
             d = partner(i)
-            greeted_copy(aligned((q * devices + d) * message, message), to, d, 0).start()
+            source = aligned(ahead + (q * devices + d) * message, message)
+            greeted_copy(source, to, d, 0).start()
             return carry
 
         lax.fori_loop(0, devices - 1, body, 0)
         pltpu.make_async_copy(
-            sending.at[aligned((q * devices + me) * message, message), :],
+            outbox.at[aligned(ahead + (q * devices + me) * message, message), :],
             arrived.at[to, :],
             recv_sem.at[0],
         ).start()
 
     def send_part(q, r, sem):
-        def cut(first, h):
-            return aligned(first * message + h * unit + r * small, small)
+        def cut(first, h, shift=0):
+            return aligned(shift + first * message + h * unit + r * small, small)
 
         def body(i, carry):
             d = partner(i)
             for h in range(PAIR):
                 greeted_copy(
-                    cut(q * devices + d, h), cut(me * pairs + q, h), d, sem
+                    cut(q * devices + d, h, ahead), cut(me * pairs + q, h), d, sem
                 ).start()
             return carry
 
         lax.fori_loop(0, devices - 1, body, 0)
         for h in range(PAIR):
             pltpu.make_async_copy(
-                sending.at[cut(q * devices + me, h), :],
+                outbox.at[cut(q * devices + me, h, ahead), :],
                 arrived.at[cut(me * pairs + q, h), :],
                 recv_sem.at[sem],
             ).start()
@@ -372,8 +374,8 @@
         got = dot3((high[at, :], low[at, :]), (rows_h[...], rows_l[...]), NT)
         for d in range(devices):
             for h in range(PAIR):
-                to = (q * devices + d) * message + h * unit + r * small
-                sending[aligned(to, small), :] = got[
+                to = ahead + (q * devices + d) * message + h * unit + r * small
+                outbox[aligned(to, small), :] = got[
                     d * small : (d + 1) * small, h * lats : (h + 1) * lats
                 ]
 
@@ -471,8 +473,18 @@
 
     def send2_copy(s, d, sem):
         return pltpu.make_async_remote_copy(
-            src_ref=synth.at[aligned((s * devices + d) * each, each), :],
+            src_ref=outbox.at[aligned((s * devices + d) * each, each), :],
             dst_ref=returned.at[me, aligned(s * each, each), :],
+            send_sem=send2_sem,
+            recv_sem=recv2_sem.at[sem],
+            device_id=mesh_id(d),
+            device_id_type=pl.DeviceIdType.MESH,
+        )
+
+    def send2_tail(s, d, sem):
+        return pltpu.make_async_remote_copy(
+            src_ref=outbox.at[aligned((s * devices + d) * each, each), :],
+            dst_ref=forced.at[wide, aligned(lax.rem(me, quarter) * GROUP * each + (s - (slots - GROUP)) * each, each), :],
             send_sem=send2_sem,
             recv_sem=recv2_sem.at[sem],
             device_id=mesh_id(d),
@@ -530,18 +542,35 @@
         first, second = both[: 2 * every], both[2 * every :]
         north, other = first + second, first - second
         base = s * devices * each
+
+        @pl.when(s == slots // 2)
+        def _():
+            sent = outbox.at[pl.ds(ahead, pairs * (devices - 1) * message), :]
+            pltpu.make_async_copy(sent, sent, send_sem).wait()
+
         for b in range(folds):
             cut = slice(b * LANES, (b + 1) * LANES)
-            synth[aligned(base + b * 2 * every, 2 * every), :] = north[:, cut]
-            synth[aligned(base + (bands - 1 - b) * 2 * every, 2 * every), :] = other[:, cut]
+            outbox[aligned(base + b * 2 * every, 2 * every), :] = north[:, cut]
+            outbox[aligned(base + (bands - 1 - b) * 2 * every, 2 * every), :] = other[:, cut]
 
         def body(i, c):
-            send2_copy(s, partner(i), sem).start()
+            d = partner(i)
+            near = senders(d // quarter)[3] == me // quarter
+            ends = jnp.logical_and(s >= slots - GROUP, near)
+
+            @pl.when(ends)
+            def _():
+                send2_tail(s, d, sem).start()
+
+            @pl.when(jnp.logical_not(ends))
+            def _():
+                send2_copy(s, d, sem).start()
+
             return c
 
         lax.fori_loop(0, devices - 1, body, 0)
         pltpu.make_async_copy(
-            synth.at[aligned((s * devices + me) * each, each), :],
+            outbox.at[aligned((s * devices + me) * each, each), :],
             returned.at[me, aligned(s * each, each), :],
             recv2_sem.at[sem],
         ).start()
@@ -557,6 +586,12 @@
 
     def landed(c, g):
         return returned.at[aligned(order[c] * quarter, quarter), g * rows : (g + 1) * rows, :]
+
+    at = aligned((groups - 1) * tall + order[3] * piece, piece)
+    for e, part in enumerate((high, low)):
+        for i in range(wide):
+            to = slice((e * wide + i) * piece, (e * wide + i + 1) * piece)
+            forced[wide + 1, to, :] = part[at, i * LANES : (i + 1) * LANES].astype(jnp.float32)
 
     for number, units in enumerate(ARRIVALS):
         copies = []
@@ -625,18 +660,15 @@
 
     for s in range(max(slots - 2, 0), slots):
         pltpu.make_async_copy(spec.at[s % 2], spec_out.at[s], spec_sem.at[s % 2]).wait()
-    sent = pl.ds(0, pairs * (devices - 1) * message)
-    pltpu.make_async_copy(sending.at[sent, :], sending.at[sent, :], send_sem).wait()
-    sent = pl.ds(0, slots * (devices - 1) * each)
-    pltpu.make_async_copy(synth.at[sent, :], synth.at[sent, :], send2_sem).wait()
-    final = landed(3, groups - 1)
-    pltpu.make_async_copy(final, final, recv2_sem.at[order[3] * groups + groups - 1]).wait()
+    sent = outbox.at[pl.ds(0, slots * (devices - 1) * each), :]
+    pltpu.make_async_copy(sent, sent, send2_sem).wait()
+    tail = forced.at[wide, pl.ds(0, quarter * rows), :]
+    pltpu.make_async_copy(tail, tail, recv2_sem.at[order[3] * groups + groups - 1]).wait()
 
 
 def finish_kernel(
-    dims, returned, partial, spectral, slot_ref, grid_out, spec_out,
-    pulled, turned, stacked, table, result, spec, wave_own, waves,
-    pull_sem, out_sem, spec_in, spec_done,
+    dims, partial, spectral, grid_out, spec_out,
+    table, turned, stacked, result, spec, out_sem, spec_in, spec_done,
 ):
     bands, parts, lats, levels, longitudes, slots, depth, half = dims
     devices = bands * parts
@@ -653,40 +685,28 @@
             out_sem.at[slot],
         )
 
-    quarter = devices // 4
-    me = lax.axis_index("band") * parts + lax.axis_index("lev")
-    first = senders(me // quarter)[3] * quarter
-    rows = GROUP * each
-    pull = pltpu.make_async_copy(
-        returned.at[aligned(first, quarter), slots * each - rows : slots * each, :], pulled, pull_sem
-    )
-    pull.start()
     spec_copy = pltpu.make_async_copy(spectral, spec, spec_in)
     spec_copy.start()
 
-    wave_columns(slot_ref, wave_own)
-    for i in range(GROUP):
-        x = wave_own[pl.ds(first * slots + slots - GROUP + i, quarter, stride=slots), :]
-        for c in range(2):
-            waves[pl.ds(2 * i + c, quarter, stride=2 * GROUP), :] = x
-    imaginary = (lax.broadcasted_iota(jnp.int32, waves.shape, 0) & 1) == 1
-    short = quarter * 2 * GROUP
-    for i, (h, l) in enumerate(table_rows(waves[...], imaginary, longitudes)):
+    for l in range(levels):
+        x = partial[wide, pl.ds(l, LANES // 2, stride=levels), :]
+        turned[pl.ds(l, lats, stride=levels), :] = jnp.concatenate([x, x], axis=0).T
+    keep = lax.broadcasted_iota(jnp.int32, (levels, LANES), 1) < LANES // 2
+    piece = LANES // 2
+    for i in range(wide):
         cut = slice(i * LANES, (i + 1) * LANES)
-        table[0:short, cut] = h
-        table[short : 2 * short, cut] = l
-        table[2 * short : 3 * short, cut] = h
-        table[3 * short : 4 * short, cut] = jnp.zeros_like(h)
+        h, l = [
+            partial[wide + 1, (e * wide + i) * piece : (e * wide + i + 1) * piece, :].astype(
+                jnp.bfloat16
+            )
+            for e in range(2)
+        ]
+        for e, part in enumerate((h, l, h, jnp.zeros_like(h))):
+            table[e * piece : (e + 1) * piece, cut] = part
+
     spec_copy.wait()
     done = pltpu.make_async_copy(spec, spec_out, spec_done)
     done.start()
-    pull.wait()
-    flat = pulled.reshape(quarter * rows, lats)
-    for l in range(levels):
-        x = flat[pl.ds(l, LANES // 2, stride=levels), :]
-        turned[pl.ds(l, lats, stride=levels), :] = jnp.concatenate([x, x], axis=0).T
-    keep = lax.broadcasted_iota(jnp.int32, (levels, LANES), 1) < LANES // 2
-
     burst = 8
 
     def split(i, carry):
@@ -741,7 +761,7 @@
         lats == LANES and levels == 2 * SUB and 4 * devices == LANES
         and longitudes % (2 * LANES) == 0 and longitudes & (longitudes - 1) == 0
         and bands % 2 == 0 and half == bands // 2 * lats and depth % LANES == 0
-        and slots == 4 * GROUP and devices * slots % LANES == 0 and levels // PAIR >= 3 and 2 * every == LANES and to_modes.shape[0] == every
+        and slots == 4 * GROUP and devices * slots % LANES == 0 and levels // PAIR >= 3 and longitudes <= lats * levels and 2 * every == LANES and to_modes.shape[0] == every
     )
     if not fits:
         return plain_shards(
@@ -758,12 +778,12 @@
     numbers = slot_wavenumber.reshape(-1, LANES)
     state = spectral_state.transpose(0, 2, 3, 1).reshape(slots, 2 * every, depth)
     square = pltpu.VMEM((2 * every, 2 * every), f32)
-    spectral, returned, partial = pl.pallas_call(
+    spectral, _, partial = pl.pallas_call(
         functools.partial(forward_kernel, dims),
         out_shape=(
             jax.ShapeDtypeStruct((slots, 2 * every, depth), f32),
             jax.ShapeDtypeStruct((devices, slots * 2 * levels, lats), f32),
-            pltpu.VMEM((wide, lats * levels, LANES), f32),
+            pltpu.VMEM((wide + 2, lats * levels, LANES), f32),
         ),
         in_specs=[hbm] * 8,
         out_specs=(hbm, hbm, vmem),
@@ -774,9 +794,8 @@
             pltpu.VMEM((2, lats // PIECES, SUB, longitudes), f32),
             pltpu.VMEM((PAIR * lats, longitudes), bf16),
             pltpu.VMEM((PAIR * lats, longitudes), bf16),
+            pltpu.VMEM((levels * count * 3 // 2, lats), f32),
             pltpu.VMEM((levels * count, lats), f32),
-            pltpu.VMEM((levels * count, lats), f32),
-            pltpu.VMEM((count * levels, lats), f32),
             pltpu.VMEM((2, depth, half), f32),
             pltpu.VMEM((2, 2 * every, depth), f32),
             pltpu.VMEM((2, 2 * every, depth), f32),
@@ -808,22 +827,19 @@
             jax.ShapeDtypeStruct(grid_adjoint.shape, f32),
             jax.ShapeDtypeStruct(spectral.shape, f32),
         ),
-        in_specs=[hbm, vmem, hbm, vmem],
+        in_specs=[vmem, hbm],
         out_specs=(hbm, hbm),
         scratch_shapes=[
-            pltpu.VMEM((devices // 4, GROUP * 2 * levels, lats), f32),
+            pltpu.VMEM((2 * LANES, longitudes), bf16),
             pltpu.VMEM((lats * levels, LANES), f32),
             pltpu.VMEM((lats * levels, 2 * LANES), bf16),
-            pltpu.VMEM((2 * LANES, longitudes), bf16),
             pltpu.VMEM((2, lats, levels, 2 * LANES), f32),
             pltpu.VMEM(spectral.shape, f32),
-            pltpu.VMEM((devices * slots, LANES), jnp.int32),
-            pltpu.VMEM((LANES // 2, LANES), jnp.int32),
-            dma, dma((2,)), dma, dma,
+            dma((2,)), dma, dma,
         ],
         compiler_params=pltpu.CompilerParams(vmem_limit_bytes=LAST_GRANT),
         name="finish",
-    )(returned, pltpu.with_memory_space_constraint(partial, pltpu.VMEM), spectral, numbers)
+    )(pltpu.with_memory_space_constraint(partial, pltpu.VMEM), spectral)
     return spectral.reshape(slots, 2, every, depth).transpose(0, 3, 1, 2), grid
 
 

time: 388 us -> 388 us (level)
  no operation moved by 1% of the time
where the time goes in v7:
time: 388 us; the launch traced here: 387 us
  Pallas kernels  386 us (99%)
    pallas_call x1, Pallas kernels, shards(): pl.pallas_call(functools.partial(forward_kernel, dims), out_shape=(jax.Sh...  375 us
    pallas_call x1, Pallas kernels, shards(): pl.pallas_call(functools.partial(finish_kernel, dims), out_shape=(jax.Sha...  11 us

profile of v7, /device:TPU:0, one launch (start us, length us, event | category | flops | bytes accessed | tf_op | source)
XLA Modules:
  0.0 386.9 jit_solution(18320290082632432029)
XLA Ops:
  0.6 375.2 %spectral.1 = (f32[16,128,512]{2,1,0:T(8,128)}, f32[32,512,128]{2,1,0:T(8,128)}, f32[18,2048,128]{2,1,0:T(8,128)S(1)}) custom-call(f32[128,16,2048]{2,1,0:T(8,128)} %grid_ref.1, f32[128,16,2048]{2,1,0:T(8,128)} %traj_ref.1, s32[4,128]{1,0:T(4,128)} %bitcast.9, f32[16,512,512]{2,1,0:T(8,128)} %leg_ref.1, f32[16,128,512]{2,1,0:T(8,128)} %bitcast.8, ...), custom_call_target="tpu_custom_call" | custom-call | tf_op jit(solution)/shard_map/spectral/pallas_call | solution.py:781
  375.9 11.0 %finish.1 = (f32[128,16,2048]{2,1,0:T(8,128)}, f32[16,128,512]{2,1,0:T(8,128)}) custom-call(f32[18,2048,128]{2,1,0:T(8,128)S(1)} %get-tuple-element.6.partial, f32[16,128,512]{2,1,0:T(8,128)} %get-tuple-element.7.spectral), custom_call_target="tpu_custom_call" | custom-call | tf_op jit(solution)/shard_map/finish/pallas_call | solution.py:824
